TPU v7x, 256 devices: a whole 4x4x8 slice. The times are simulated.
256 devices in a mesh: depth: 64 (over z, y, core), tile: 4 (over x).
Axes of the slice: x: 4, y: 4, z: 8, core: 2. Of those that a mesh axis runs over, the one named last changes fastest.
Arguments:
- density: float32 [128, 512, 2048], P('depth', 'tile'), may hold values from -6 to 6
- bins: int32 [128, 512, 2048], P('depth', 'tile'), may hold values from 0 to 255
- colors: bfloat16 [3, 256], replicated, may hold values from 0.099609375 to 1
- extinction: bfloat16 [256], replicated, may hold values from 0.049804688 to 20
Outputs:
- image: float32 [4, 512, 2048], P(None, 'tile', 'depth')
All inputs are finite; a program needn't handle non-finite values.
Results may differ from a plain program's by a relative error of at most 0.0003.
Values sent between devices are 32-bit elements; how exact they have to be, the bound alone decides.
A program may use at most 256 MiB of HBM per device.

v0:
```python
import math

import jax
import jax.numpy as jnp
from jax import lax
from jax.sharding import PartitionSpec as P


def padded_2(cells, sides, width):
    for axis, dim in sides:
        count = lax.axis_size(axis)
        ends = count - 1
        head = lax.slice_in_dim(cells, 0, width, axis=dim)
        tail = lax.slice_in_dim(cells, cells.shape[dim] - width, cells.shape[dim], axis=dim)
        cells = jnp.concatenate(
            [
                lax.ppermute(tail, axis, [(i, (i + 1) % count) for i in range(ends)]),
                cells,
                lax.ppermute(head, axis, [((i + 1) % count, i) for i in range(ends)]),
            ],
            axis=dim,
        )
    return cells


def partner(value, axis, stride):
    return lax.ppermute(value, axis, [(i, i ^ 1 << stride) for i in range(lax.axis_size(axis))])


def over_pair(front, back):
    return jnp.concatenate([front[:3] + front[3:] * back[:3], front[3:] * back[3:]], 0)


def per_device(density, bins, colors, extinction):
    depth_cells, row_cells, col_cells = density.shape
    slab_count = lax.axis_size("depth")
    depth_scale = 0.6 / (depth_cells * slab_count)
    padded = padded_2(density, (("depth", 0), ("tile", 1)), 1)
    grad_x = (padded[2:, 1:-1] - padded[:-2, 1:-1]) * 0.5
    grad_y = (padded[1:-1, 2:] - padded[1:-1, :-2]) * 0.5
    col_pad = jnp.pad(density, ((0, 0), (0, 0), (1, 1)))
    grad_z = (col_pad[:, :, 2:] - col_pad[:, :, :-2]) * 0.5
    lit = jnp.abs(0.48 * grad_x + 0.6 * grad_y + 0.64 * grad_z)
    shade = 0.3 + 0.7 * lit / jnp.sqrt(grad_x * grad_x + grad_y * grad_y + grad_z * grad_z + 1.0)
    lookup = jnp.concatenate([colors, extinction[None, :]], 0)
    entry_count = lookup.shape[1]
    low_count = 16
    high_count = entry_count // low_count
    table_rows = lookup.reshape(4, high_count, low_count).reshape(4 * high_count, low_count)
    total_cells = depth_cells * row_cells * col_cells
    block_size = math.gcd(total_cells, 32768)
    low_levels = lax.iota(jnp.int32, low_count)[:, None]
    high_levels = lax.iota(jnp.int32, high_count)[:, None]

    def look_block(bin_block):
        low_digit = bin_block % low_count
        high_digit = bin_block // low_count
        onehot_low = (low_levels == low_digit[None, :]).astype(jnp.bfloat16)
        partial_rows = jnp.dot(table_rows, onehot_low, preferred_element_type=jnp.float32)
        partial_rows = partial_rows.reshape(4, high_count, bin_block.shape[0])
        onehot_high = (high_levels == high_digit[None, :]).astype(jnp.float32)
        return jnp.sum(partial_rows * onehot_high[None], axis=1)

    entries = lax.map(look_block, bins.reshape(-1, block_size))
    entries = jnp.moveaxis(entries, 1, 0).reshape(4, depth_cells, row_cells, col_cells)
    optical = entries[3] * depth_scale
    emitted = entries[:3] * shade * (1.0 - jnp.exp(-optical))
    running = jnp.cumsum(optical, axis=0)
    radiance = jnp.sum(jnp.exp(-(running - optical)) * emitted, axis=1)
    transmit = jnp.exp(-running[-1])
    image_part = jnp.concatenate([radiance, transmit[None]], 0)
    slab_index = lax.axis_index("depth")
    for round_index in range(slab_count.bit_length() - 1):
        half_width = image_part.shape[2] // 2
        lower_part = image_part[:, :, :half_width]
        upper_part = image_part[:, :, half_width:]
        behind = jnp.right_shift(slab_index, round_index) % 2 == 1
        kept_part = jnp.where(behind, upper_part, lower_part)
        sent_part = jnp.where(behind, lower_part, upper_part)
        received = partner(sent_part, "depth", round_index)
        front = jnp.where(behind, received, kept_part)
        back = jnp.where(behind, kept_part, received)
        image_part = over_pair(front, back)
    return jnp.concatenate([image_part[:3], 1.0 - image_part[3:]], 0)


def solution(mesh):
    return jax.shard_map(
        per_device,
        mesh=mesh,
        in_specs=(P("depth", "tile", None), P("depth", "tile", None), P(), P()),
        out_specs=P(None, "tile", "depth"),
        check_vma=False,
    )
```

profile of v0, /device:TPU:8, one launch (start us, length us, event | category | flops | bytes accessed | tf_op | source)
XLA Modules:
  0.0 220.3 jit_solution(1524842501735338716)
XLA Ops:
  0.0 3.1 %fusion.24 = (f32[1,128,2048]{2,1,0:T(8,128)}, f32[1,128,2048]{2,1,0:T(8,128)}) fusion(f32[2,128,2048]{2,1,0:T(8,128)} %param.6), kind=kLoop, calls=%fused_computation.109 | loop fusion | bytes 4194304 | tf_op jit(solution)/shard_map/slice | solution.py:13
  3.1 1.9 collective-permute-start
  5.1 2.4 %collective-permute-start.1 = (f32[1,128,2048]{2,1,0:T(8,128)}, f32[1,128,2048]{2,1,0:T(8,128)}, u32[]{:S(2)}, u32[]{:S(2)}) collective-permute-start(f32[1,128,2048]{2,1,0:T(8,128)} %get-tuple-element.152), channel_id=1, source_target_pairs={{0,4},{4,8},{8,12},{12,16},{16,20},{20,24},{24,28},{28,32},{32,36}... | collective-permute-start | bytes 3145736 | tf_op jit(solution)/shard_map/ppermute | solution.py:17
  7.7 1.8 reshape.70
  9.5 71.7 %while.15 = (s32[]{:T(128)}, f32[16,4,32768]{2,1,0:T(4,128)}, s32[16,32768]{1,0:T(8,128)S(1)}, bf16[64,16]{0,1:T(8,128)(2,1)S(1)}, s32[]{:T(128)}) while((s32[]{:T(128)}, f32[16,4,32768]{2,1,0:T(4,128)}, s32[16,32768]{1,0:T(8,128)S(1)}, bf16[64,16]{0,1:T(8,128)(2,1)S(1)}, s32[]{:T(128)}) %tuple.56), condition=%wide.region_2.3_spmd.clone.clone, body=%wide.region_0.2_spmd.clone.clone.sunk | while | flops 73498624 | bytes 6817873 | solution.py:64
  10.7 2.5 %multiply_reduce_fusion.3 = f32[4,32768]{1,0:T(4,128)S(1)} fusion(f32[16,32768]{1,0:T(8,128)S(1)} %fusion.31, bf16[64,16]{0,1:T(8,128)(2,1)S(1)} %get-tuple-element.213, s32[32768]{0:T(1024)S(1)} %bitcast.37), kind=kOutput, calls=%fused_computation.1.clone.1 | convolution fusion | flops 71696384 | bytes 2754560 | tf_op jit(solution)/shard_map/while/body/eval_jaxpr/dot_general | solution.py:59
  15.1 2.5 %multiply_reduce_fusion.3 = f32[4,32768]{1,0:T(4,128)S(1)} fusion(f32[16,32768]{1,0:T(8,128)S(1)} %fusion.31, bf16[64,16]{0,1:T(8,128)(2,1)S(1)} %get-tuple-element.213, s32[32768]{0:T(1024)S(1)} %bitcast.37), kind=kOutput, calls=%fused_computation.1.clone.1 | convolution fusion | flops 71696384 | bytes 2754560 | tf_op jit(solution)/shard_map/while/body/eval_jaxpr/dot_general | solution.py:59
  19.6 2.5 %multiply_reduce_fusion.3 = f32[4,32768]{1,0:T(4,128)S(1)} fusion(f32[16,32768]{1,0:T(8,128)S(1)} %fusion.31, bf16[64,16]{0,1:T(8,128)(2,1)S(1)} %get-tuple-element.213, s32[32768]{0:T(1024)S(1)} %bitcast.37), kind=kOutput, calls=%fused_computation.1.clone.1 | convolution fusion | flops 71696384 | bytes 2754560 | tf_op jit(solution)/shard_map/while/body/eval_jaxpr/dot_general | solution.py:59
  24.1 2.5 %multiply_reduce_fusion.3 = f32[4,32768]{1,0:T(4,128)S(1)} fusion(f32[16,32768]{1,0:T(8,128)S(1)} %fusion.31, bf16[64,16]{0,1:T(8,128)(2,1)S(1)} %get-tuple-element.213, s32[32768]{0:T(1024)S(1)} %bitcast.37), kind=kOutput, calls=%fused_computation.1.clone.1 | convolution fusion | flops 71696384 | bytes 2754560 | tf_op jit(solution)/shard_map/while/body/eval_jaxpr/dot_general | solution.py:59
  28.6 2.5 %multiply_reduce_fusion.3 = f32[4,32768]{1,0:T(4,128)S(1)} fusion(f32[16,32768]{1,0:T(8,128)S(1)} %fusion.31, bf16[64,16]{0,1:T(8,128)(2,1)S(1)} %get-tuple-element.213, s32[32768]{0:T(1024)S(1)} %bitcast.37), kind=kOutput, calls=%fused_computation.1.clone.1 | convolution fusion | flops 71696384 | bytes 2754560 | tf_op jit(solution)/shard_map/while/body/eval_jaxpr/dot_general | solution.py:59
  33.1 2.5 %multiply_reduce_fusion.3 = f32[4,32768]{1,0:T(4,128)S(1)} fusion(f32[16,32768]{1,0:T(8,128)S(1)} %fusion.31, bf16[64,16]{0,1:T(8,128)(2,1)S(1)} %get-tuple-element.213, s32[32768]{0:T(1024)S(1)} %bitcast.37), kind=kOutput, calls=%fused_computation.1.clone.1 | convolution fusion | flops 71696384 | bytes 2754560 | tf_op jit(solution)/shard_map/while/body/eval_jaxpr/dot_general | solution.py:59
  37.5 2.5 %multiply_reduce_fusion.3 = f32[4,32768]{1,0:T(4,128)S(1)} fusion(f32[16,32768]{1,0:T(8,128)S(1)} %fusion.31, bf16[64,16]{0,1:T(8,128)(2,1)S(1)} %get-tuple-element.213, s32[32768]{0:T(1024)S(1)} %bitcast.37), kind=kOutput, calls=%fused_computation.1.clone.1 | convolution fusion | flops 71696384 | bytes 2754560 | tf_op jit(solution)/shard_map/while/body/eval_jaxpr/dot_general | solution.py:59
  42.0 2.5 %multiply_reduce_fusion.3 = f32[4,32768]{1,0:T(4,128)S(1)} fusion(f32[16,32768]{1,0:T(8,128)S(1)} %fusion.31, bf16[64,16]{0,1:T(8,128)(2,1)S(1)} %get-tuple-element.213, s32[32768]{0:T(1024)S(1)} %bitcast.37), kind=kOutput, calls=%fused_computation.1.clone.1 | convolution fusion | flops 71696384 | bytes 2754560 | tf_op jit(solution)/shard_map/while/body/eval_jaxpr/dot_general | solution.py:59
  46.5 2.5 %multiply_reduce_fusion.3 = f32[4,32768]{1,0:T(4,128)S(1)} fusion(f32[16,32768]{1,0:T(8,128)S(1)} %fusion.31, bf16[64,16]{0,1:T(8,128)(2,1)S(1)} %get-tuple-element.213, s32[32768]{0:T(1024)S(1)} %bitcast.37), kind=kOutput, calls=%fused_computation.1.clone.1 | convolution fusion | flops 71696384 | bytes 2754560 | tf_op jit(solution)/shard_map/while/body/eval_jaxpr/dot_general | solution.py:59
  50.9 2.5 %multiply_reduce_fusion.3 = f32[4,32768]{1,0:T(4,128)S(1)} fusion(f32[16,32768]{1,0:T(8,128)S(1)} %fusion.31, bf16[64,16]{0,1:T(8,128)(2,1)S(1)} %get-tuple-element.213, s32[32768]{0:T(1024)S(1)} %bitcast.37), kind=kOutput, calls=%fused_computation.1.clone.1 | convolution fusion | flops 71696384 | bytes 2754560 | tf_op jit(solution)/shard_map/while/body/eval_jaxpr/dot_general | solution.py:59
  55.4 2.5 %multiply_reduce_fusion.3 = f32[4,32768]{1,0:T(4,128)S(1)} fusion(f32[16,32768]{1,0:T(8,128)S(1)} %fusion.31, bf16[64,16]{0,1:T(8,128)(2,1)S(1)} %get-tuple-element.213, s32[32768]{0:T(1024)S(1)} %bitcast.37), kind=kOutput, calls=%fused_computation.1.clone.1 | convolution fusion | flops 71696384 | bytes 2754560 | tf_op jit(solution)/shard_map/while/body/eval_jaxpr/dot_general | solution.py:59
  59.9 2.5 %multiply_reduce_fusion.3 = f32[4,32768]{1,0:T(4,128)S(1)} fusion(f32[16,32768]{1,0:T(8,128)S(1)} %fusion.31, bf16[64,16]{0,1:T(8,128)(2,1)S(1)} %get-tuple-element.213, s32[32768]{0:T(1024)S(1)} %bitcast.37), kind=kOutput, calls=%fused_computation.1.clone.1 | convolution fusion | flops 71696384 | bytes 2754560 | tf_op jit(solution)/shard_map/while/body/eval_jaxpr/dot_general | solution.py:59
  64.4 2.5 %multiply_reduce_fusion.3 = f32[4,32768]{1,0:T(4,128)S(1)} fusion(f32[16,32768]{1,0:T(8,128)S(1)} %fusion.31, bf16[64,16]{0,1:T(8,128)(2,1)S(1)} %get-tuple-element.213, s32[32768]{0:T(1024)S(1)} %bitcast.37), kind=kOutput, calls=%fused_computation.1.clone.1 | convolution fusion | flops 71696384 | bytes 2754560 | tf_op jit(solution)/shard_map/while/body/eval_jaxpr/dot_general | solution.py:59
  68.9 2.5 %multiply_reduce_fusion.3 = f32[4,32768]{1,0:T(4,128)S(1)} fusion(f32[16,32768]{1,0:T(8,128)S(1)} %fusion.31, bf16[64,16]{0,1:T(8,128)(2,1)S(1)} %get-tuple-element.213, s32[32768]{0:T(1024)S(1)} %bitcast.37), kind=kOutput, calls=%fused_computation.1.clone.1 | convolution fusion | flops 71696384 | bytes 2754560 | tf_op jit(solution)/shard_map/while/body/eval_jaxpr/dot_general | solution.py:59
  73.3 2.5 %multiply_reduce_fusion.3 = f32[4,32768]{1,0:T(4,128)S(1)} fusion(f32[16,32768]{1,0:T(8,128)S(1)} %fusion.31, bf16[64,16]{0,1:T(8,128)(2,1)S(1)} %get-tuple-element.213, s32[32768]{0:T(1024)S(1)} %bitcast.37), kind=kOutput, calls=%fused_computation.1.clone.1 | convolution fusion | flops 71696384 | bytes 2754560 | tf_op jit(solution)/shard_map/while/body/eval_jaxpr/dot_general | solution.py:59
  77.8 2.5 %multiply_reduce_fusion.3 = f32[4,32768]{1,0:T(4,128)S(1)} fusion(f32[16,32768]{1,0:T(8,128)S(1)} %fusion.31, bf16[64,16]{0,1:T(8,128)(2,1)S(1)} %get-tuple-element.213, s32[32768]{0:T(1024)S(1)} %bitcast.37), kind=kOutput, calls=%fused_computation.1.clone.1 | convolution fusion | flops 71696384 | bytes 2754560 | tf_op jit(solution)/shard_map/while/body/eval_jaxpr/dot_general | solution.py:59
  81.2 10.2 %fusion.9 = f32[16,32768]{1,0:T(8,128)S(1)} fusion(f32[4,16,32768]{2,0,1:T(4,128)} %bitcast.35), kind=kLoop, calls=%fused_computation.28 | loop fusion | flops 524288 | bytes 4194304 | tf_op jit(solution)/shard_map/mul | solution.py:66
  91.4 1.5 mul.181
  92.9 1.9 copy.25
  95.4 1.9 negate_exponential_fusion
  97.3 1.6 exponential_subtract_fusion
  98.9 1.4 constant_dynamic-update-slice_fusion.2
  102.4 4.5 %collective-permute-start.3 = (f32[4,1,2048]{2,1,0:T(1,128)S(1)}, f32[4,1,2048]{2,1,0:T(1,128)S(1)}, u32[]{:S(2)}, u32[]{:S(2)}) collective-permute-start(f32[4,1,2048]{2,1,0:T(1,128)S(1)} %get-tuple-element.146), channel_id=1, source_target_pairs={{0,1},{1,2},{2,3},{4,5},{5,6},{6,7},{8,9},{9,10},{10,11},{12,13},{... | collective-permute-start | bytes 98312 | tf_op jit(solution)/shard_map/ppermute | solution.py:17
  108.1 2.9 %copy.27 = f32[2,128,2048]{2,1,0:T(8,128)} copy(f32[2,128,2048]{1,2,0:T(8,128)} %negate_exponential_fusion) | data formatting | bytes 4194304 | tf_op jit(solution)/shard_map/exp | solution.py:69
  111.0 9.7 %copy.28 = f32[3,16,32768]{2,1,0:T(8,128)} copy(f32[3,16,32768]{2,0,1:T(4,128)} %bitcast.36) | data formatting | bytes 12582912 | tf_op jit(solution)/shard_map/slice | solution.py:67
  120.8 7.2 %slice.163 = f32[3,2,128,2048]{3,2,1,0:T(8,128)} reshape(f32[3,16,32768]{2,1,0:T(8,128)} %copy.28) | data formatting | bytes 12582912 | tf_op jit(solution)/shard_map/slice | solution.py:67
  128.0 4.1 %multiply_add_fusion = f32[2,128,2048]{2,1,0:T(8,128)S(1)} fusion(f32[2,128,2048]{2,1,0:T(8,128)S(1)} %copy-done.1, f32[4,128,2048]{2,1,0:T(8,128)} %copy-done.3, f32[4,1,2048]{2,1,0:T(1,128)S(1)} %collective-permute-done.3, f32[4,1,2048]{2,1,0:T(1,128)S(1)} %collective-permute-done.2, f32[1,128,2048]{2,1,0:T(8,128)} %collective-permute-done.1, ...), kind=kLoop, calls=%fused_computation.32 | loop fusion | flops 13107200 | bytes 10551296 | tf_op jit(solution)/shard_map/add | solution.py:44
  132.3 5.9 %multiply_reduce_fusion.1 = f32[3,128,2048]{2,1,0:T(8,128)} fusion(f32[3,2,128,2048]{3,2,1,0:T(8,128)S(1)} %copy-done, f32[2,128,2048]{2,1,0:T(8,128)} %exponential_subtract_fusion, f32[2,128,2048]{2,1,0:T(8,128)S(1)} %multiply_add_fusion, f32[2,128,2048]{2,1,0:T(8,128)} %copy.27), kind=kLoop, calls=%fused_computation.13 | loop fusion | flops 5505024 | bytes 15728640 | tf_op jit(solution)/shard_map/reduce_sum | solution.py:69
  138.2 2.4 %copy.29 = f32[3,128,2048]{1,2,0:T(8,128)S(1)} copy(f32[3,128,2048]{2,1,0:T(8,128)} %multiply_reduce_fusion.1) | data formatting | bytes 6291456 | tf_op jit(solution)/shard_map/reduce_sum | solution.py:69
  140.6 2.7 %broadcast_select_fusion.3 = f32[4,128,1024]{1,2,0:T(8,128)} fusion(pred[]{:T(512)S(6)} %eq.103, f32[1,128,2048]{1,2,0:T(8,128)} %fusion.12, f32[3,128,2048]{1,2,0:T(8,128)S(1)} %copy.29), kind=kLoop, calls=%fused_computation.45 | loop fusion | flops 1572864 | bytes 6291457 | tf_op jit(solution)/shard_map/jit(_where)/select_n | solution.py:79
  143.9 4.1 %collective-permute-done.4 = f32[4,128,1024]{1,2,0:T(8,128)} collective-permute-done((f32[4,128,1024]{1,2,0:T(8,128)}, f32[4,128,1024]{1,2,0:T(8,128)}, u32[]{:S(2)}, u32[]{:S(2)}) %collective-permute-start.4) | collective-permute-done | bytes 2097184 | tf_op jit(solution)/shard_map/ppermute | solution.py:27
  148.1 2.4 %broadcast_select_fusion.1 = (f32[4,128,1024]{1,2,0:T(8,128)S(1)}, f32[4,128,1024]{1,2,0:T(8,128)S(1)}) fusion(f32[4,128,1024]{1,2,0:T(8,128)} %collective-permute-done.4, pred[]{:T(512)S(6)} %eq.103, f32[1,128,2048]{1,2,0:T(8,128)} %fusion.12, f32[3,128,2048]{1,2,0:T(8,128)S(1)} %copy.29), kind=kLoop, calls=%fused_computation.43 | loop fusion | flops 3670016 | bytes 10485761 | tf_op jit(solution)/shard_map/jit(_where)/select_n | solution.py:81
  150.8 3.0 %collective-permute-start.5 = (f32[4,128,512]{1,2,0:T(8,128)S(1)}, f32[4,128,512]{1,2,0:T(8,128)}, u32[]{:S(2)}, u32[]{:S(2)}) collective-permute-start(f32[4,128,512]{1,2,0:T(8,128)S(1)} %broadcast_select_fusion.7), channel_id=1, source_target_pairs={{0,8},{4,12},{8,0},{12,4},{16,24},{20,28},{24,16},{28,20},{32,40},... | collective-permute-start | bytes 3145736 | tf_op jit(solution)/shard_map/ppermute | solution.py:27
  153.8 23.6 %collective-permute-done.5 = f32[4,128,512]{1,2,0:T(8,128)} collective-permute-done((f32[4,128,512]{1,2,0:T(8,128)S(1)}, f32[4,128,512]{1,2,0:T(8,128)}, u32[]{:S(2)}, u32[]{:S(2)}) %collective-permute-start.5) | collective-permute-done | bytes 1048608 | tf_op jit(solution)/shard_map/ppermute | solution.py:27
  177.4 1.4 broadcast_select_fusion.5
  179.0 3.5 %collective-permute-start.6 = (f32[4,128,256]{1,2,0:T(8,128)S(1)}, f32[4,128,256]{1,2,0:T(8,128)S(1)}, u32[]{:S(2)}, u32[]{:S(2)}) collective-permute-start(f32[4,128,256]{1,2,0:T(8,128)S(1)} %broadcast_select_fusion.11), channel_id=1, source_target_pairs={{0,16},{4,20},{8,24},{12,28},{16,0},{20,4},{24,8},{28,12},{32,48},... | collective-permute-start | bytes 1572872 | tf_op jit(solution)/shard_map/ppermute | solution.py:27
  182.5 11.6 %collective-permute-done.6 = f32[4,128,256]{1,2,0:T(8,128)S(1)} collective-permute-done((f32[4,128,256]{1,2,0:T(8,128)S(1)}, f32[4,128,256]{1,2,0:T(8,128)S(1)}, u32[]{:S(2)}, u32[]{:S(2)}) %collective-permute-start.6) | collective-permute-done | bytes 524320 | tf_op jit(solution)/shard_map/ppermute | solution.py:27
  194.3 2.0 collective-permute-start.7
  196.3 5.4 %collective-permute-done.7 = f32[4,128,128]{1,2,0:T(8,128)S(1)} collective-permute-done((f32[4,128,128]{1,2,0:T(8,128)S(1)}, f32[4,128,128]{1,2,0:T(8,128)S(1)}, u32[]{:S(2)}, u32[]{:S(2)}) %collective-permute-start.7) | collective-permute-done | bytes 262176 | tf_op jit(solution)/shard_map/ppermute | solution.py:27
  201.9 4.6 %collective-permute-start.8 = (f32[4,128,64]{1,2,0:T(8,128)S(1)}, f32[4,128,64]{1,2,0:T(8,128)S(1)}, u32[]{:S(2)}, u32[]{:S(2)}) collective-permute-start(f32[4,128,64]{1,2,0:T(8,128)S(1)} %broadcast_select_fusion.19), channel_id=1, source_target_pairs={{0,64},{4,68},{8,72},{12,76},{16,80},{20,84},{24,88},{28,92},{32,9... | collective-permute-start | bytes 393224 | tf_op jit(solution)/shard_map/ppermute | solution.py:27
  206.5 4.8 %collective-permute-done.8 = f32[4,128,64]{1,2,0:T(8,128)S(1)} collective-permute-done((f32[4,128,64]{1,2,0:T(8,128)S(1)}, f32[4,128,64]{1,2,0:T(8,128)S(1)}, u32[]{:S(2)}, u32[]{:S(2)}) %collective-permute-start.8) | collective-permute-done | bytes 131104 | tf_op jit(solution)/shard_map/ppermute | solution.py:27
  211.3 5.1 %collective-permute-start.9 = (f32[4,128,32]{1,2,0:T(8,128)S(1)}, f32[4,128,32]{1,2,0:T(8,128)S(1)}, u32[]{:S(2)}, u32[]{:S(2)}) collective-permute-start(f32[4,128,32]{1,2,0:T(8,128)S(1)} %broadcast_select_fusion.23), channel_id=1, source_target_pairs={{0,128},{4,132},{8,136},{12,140},{16,144},{20,148},{24,152},{28,15... | collective-permute-start | bytes 196616 | tf_op jit(solution)/shard_map/ppermute | solution.py:27
  216.5 3.1 %collective-permute-done.9 = f32[4,128,32]{1,2,0:T(8,128)S(1)} collective-permute-done((f32[4,128,32]{1,2,0:T(8,128)S(1)}, f32[4,128,32]{1,2,0:T(8,128)S(1)}, u32[]{:S(2)}, u32[]{:S(2)}) %collective-permute-start.9) | collective-permute-done | bytes 65568 | tf_op jit(solution)/shard_map/ppermute | solution.py:27
  (114 shorter events, 38.1 us)
Async XLA Ops:
  0.0 7.5 %copy-start.5 = (bf16[256]{0:T(256)(128)(2,1)S(1)}, bf16[256]{0:T(256)(128)(2,1)}, u32[]{:S(2)}) copy-start(bf16[256]{0:T(256)(128)(2,1)} %param.9) | copy-start | bytes 1540
  0.0 7.5 %copy-start.4 = (bf16[3,256]{1,0:T(4,128)(2,1)S(1)}, bf16[3,256]{1,0:T(4,128)(2,1)}, u32[]{:S(2)}) copy-start(bf16[3,256]{1,0:T(4,128)(2,1)} %param.8) | copy-start | bytes 4612
  3.1 97.8 %collective-permute-start = (f32[1,128,2048]{2,1,0:T(8,128)}, f32[1,128,2048]{2,1,0:T(8,128)S(1)}, u32[]{:S(2)}, u32[]{:S(2)}) collective-permute-start(f32[1,128,2048]{2,1,0:T(8,128)} %get-tuple-element.151), channel_id=1, source_target_pairs={{4,0},{8,4},{12,8},{16,12},{20,16},{24,20},{28,24},{32,28},{36,32}... | collective-permute-start | bytes 3145736 | tf_op jit(solution)/shard_map/ppermute | solution.py:19
  5.1 93.8 %collective-permute-start.1 = (f32[1,128,2048]{2,1,0:T(8,128)}, f32[1,128,2048]{2,1,0:T(8,128)}, u32[]{:S(2)}, u32[]{:S(2)}) collective-permute-start(f32[1,128,2048]{2,1,0:T(8,128)} %get-tuple-element.152), channel_id=1, source_target_pairs={{0,4},{4,8},{8,12},{12,16},{16,20},{20,24},{24,28},{28,32},{32,36}... | collective-permute-start | bytes 3145736 | tf_op jit(solution)/shard_map/ppermute | solution.py:17
  95.3 1.9 copy-start.2
  98.8 1.9 copy-start.1
  101.0 7.1 %copy-start.3 = (f32[4,128,2048]{2,1,0:T(8,128)}, f32[4,128,2048]{2,1,0:T(8,128)S(1)}, u32[]{:S(2)}) copy-start(f32[4,128,2048]{2,1,0:T(8,128)S(1)} %constant_dynamic-update-slice_fusion) | copy-start | bytes 12582916
  101.1 26.9 %collective-permute-start.2 = (f32[4,1,2048]{2,1,0:T(1,128)S(1)}, f32[4,1,2048]{2,1,0:T(1,128)S(1)}, u32[]{:S(2)}, u32[]{:S(2)}) collective-permute-start(f32[4,1,2048]{2,1,0:T(1,128)S(1)} %get-tuple-element.145), channel_id=1, source_target_pairs={{1,0},{2,1},{3,2},{5,4},{6,5},{7,6},{9,8},{10,9},{11,10},{13,12},{... | collective-permute-start | bytes 98312 | tf_op jit(solution)/shard_map/ppermute | solution.py:19
  102.4 25.6 %collective-permute-start.3 = (f32[4,1,2048]{2,1,0:T(1,128)S(1)}, f32[4,1,2048]{2,1,0:T(1,128)S(1)}, u32[]{:S(2)}, u32[]{:S(2)}) collective-permute-start(f32[4,1,2048]{2,1,0:T(1,128)S(1)} %get-tuple-element.146), channel_id=1, source_target_pairs={{0,1},{1,2},{2,3},{4,5},{5,6},{6,7},{8,9},{9,10},{10,11},{12,13},{... | collective-permute-start | bytes 98312 | tf_op jit(solution)/shard_map/ppermute | solution.py:17
  128.0 4.4 %copy-start = (f32[3,2,128,2048]{3,2,1,0:T(8,128)S(1)}, f32[3,2,128,2048]{3,2,1,0:T(8,128)}, u32[]{:S(2)}) copy-start(f32[3,2,128,2048]{3,2,1,0:T(8,128)} %slice.163) | copy-start | bytes 18874372
  143.3 4.8 %collective-permute-start.4 = (f32[4,128,1024]{1,2,0:T(8,128)}, f32[4,128,1024]{1,2,0:T(8,128)}, u32[]{:S(2)}, u32[]{:S(2)}) collective-permute-start(f32[4,128,1024]{1,2,0:T(8,128)} %broadcast_select_fusion.3), channel_id=1, source_target_pairs={{0,4},{4,0},{8,12},{12,8},{16,20},{20,16},{24,28},{28,24},{32,36},... | collective-permute-start | bytes 6291464 | tf_op jit(solution)/shard_map/ppermute | solution.py:27
  150.8 26.5 %collective-permute-start.5 = (f32[4,128,512]{1,2,0:T(8,128)S(1)}, f32[4,128,512]{1,2,0:T(8,128)}, u32[]{:S(2)}, u32[]{:S(2)}) collective-permute-start(f32[4,128,512]{1,2,0:T(8,128)S(1)} %broadcast_select_fusion.7), channel_id=1, source_target_pairs={{0,8},{4,12},{8,0},{12,4},{16,24},{20,28},{24,16},{28,20},{32,40},... | collective-permute-start | bytes 3145736 | tf_op jit(solution)/shard_map/ppermute | solution.py:27
  179.0 15.1 %collective-permute-start.6 = (f32[4,128,256]{1,2,0:T(8,128)S(1)}, f32[4,128,256]{1,2,0:T(8,128)S(1)}, u32[]{:S(2)}, u32[]{:S(2)}) collective-permute-start(f32[4,128,256]{1,2,0:T(8,128)S(1)} %broadcast_select_fusion.11), channel_id=1, source_target_pairs={{0,16},{4,20},{8,24},{12,28},{16,0},{20,4},{24,8},{28,12},{32,48},... | collective-permute-start | bytes 1572872 | tf_op jit(solution)/shard_map/ppermute | solution.py:27
  194.3 7.4 %collective-permute-start.7 = (f32[4,128,128]{1,2,0:T(8,128)S(1)}, f32[4,128,128]{1,2,0:T(8,128)S(1)}, u32[]{:S(2)}, u32[]{:S(2)}) collective-permute-start(f32[4,128,128]{1,2,0:T(8,128)S(1)} %broadcast_select_fusion.15), channel_id=1, source_target_pairs={{0,32},{4,36},{8,40},{12,44},{16,48},{20,52},{24,56},{28,60},{32,0... | collective-permute-start | bytes 786440 | tf_op jit(solution)/shard_map/ppermute | solution.py:27
  201.9 9.4 %collective-permute-start.8 = (f32[4,128,64]{1,2,0:T(8,128)S(1)}, f32[4,128,64]{1,2,0:T(8,128)S(1)}, u32[]{:S(2)}, u32[]{:S(2)}) collective-permute-start(f32[4,128,64]{1,2,0:T(8,128)S(1)} %broadcast_select_fusion.19), channel_id=1, source_target_pairs={{0,64},{4,68},{8,72},{12,76},{16,80},{20,84},{24,88},{28,92},{32,9... | collective-permute-start | bytes 393224 | tf_op jit(solution)/shard_map/ppermute | solution.py:27
  211.3 8.3 %collective-permute-start.9 = (f32[4,128,32]{1,2,0:T(8,128)S(1)}, f32[4,128,32]{1,2,0:T(8,128)S(1)}, u32[]{:S(2)}, u32[]{:S(2)}) collective-permute-start(f32[4,128,32]{1,2,0:T(8,128)S(1)} %broadcast_select_fusion.23), channel_id=1, source_target_pairs={{0,128},{4,132},{8,136},{12,140},{16,144},{20,148},{24,152},{28,15... | collective-permute-start | bytes 196616 | tf_op jit(solution)/shard_map/ppermute | solution.py:27
where the time goes:
time: 222 us; the launch traced here: 220 us
  waiting for transfers between devices  52.7 us (24%)
  other arithmetic  51.7 us (23%)
  local copies, waits for them, and re-layouts  46.7 us (21%)
  matrix products  39.6 us (18%)
  starting transfers between devices  28.9 us (13%)
    ppermute x6, waiting for transfers between devices, partner(): lax.ppermute(value, axis, [(i, i ^ 1 << stride) for i in range(lax.axis_s...  52.7 us
    dot_general x16, matrix products, look_block(): jnp.dot(table_rows, onehot_low, preferred_element_type=jnp.float32)  39.6 us
    ppermute x6, starting transfers between devices, partner(): lax.ppermute(value, axis, [(i, i ^ 1 << stride) for i in range(lax.axis_s...  18.8 us
    slice x2, local copies, waits for them, and re-layouts, per_device(): emitted = entries[:3] * shade * (1.0 - jnp.exp(-optical))  16.9 us
    dynamic_update_slice x16, local copies, waits for them, and re-layouts, per_device(): entries = lax.map(look_block, bins.reshape(-1, block_size))  13.5 us
    mul x1, other arithmetic, per_device(): optical = entries[3] * depth_scale  10.2 us
    select_n x16, other arithmetic, look_block(): high_digit = bin_block // low_count  8.83 us
    select_n x16, other arithmetic, look_block(): low_digit = bin_block % low_count  7.15 us
  transfers between devices with their start and end apart: 10, of which 6 were waited for; matrix products, arithmetic and copies ran while one was open for 52% of the time, Pallas kernels for 0%

commit v1 on v0

v1 whole, which is shorter than its diff:
```python
import functools

import jax
import jax.numpy as jnp
from jax import lax
from jax.experimental import pallas as pl
from jax.experimental.pallas import tpu as pltpu
from jax.sharding import PartitionSpec as P

ROW_BLOCK = 32
LANES = 128


def shift_pair(axis, count):
    return [(i, i + 1) for i in range(count - 1)], [(i + 1, i) for i in range(count - 1)]


def partner(value, axis, stride):
    return lax.ppermute(value, axis, [(i, i ^ 1 << stride) for i in range(lax.axis_size(axis))])


def over_pair(front, back):
    return jnp.concatenate([front[:3] + front[3:] * back[:3], front[3:] * back[3:]], 0)


def render_kernel(depth_scale, table_ref, d_ref, dprev_ref, dnext_ref, htop_ref, hbot_ref,
                  xp_ref, xn_ref, b_ref, out_ref):
    block = pl.program_id(0)
    last_block = pl.num_programs(0) - 1
    chunks = d_ref.shape[1] // 8
    groups = d_ref.shape[2] // LANES
    sub = lax.broadcasted_iota(jnp.int32, (8, LANES), 0)
    lane = lax.broadcasted_iota(jnp.int32, (8, LANES), 1)
    tables = [
        (jnp.broadcast_to(table_ref[ch:ch + 1, 0:LANES], (8, LANES)),
         jnp.broadcast_to(table_ref[ch:ch + 1, LANES:2 * LANES], (8, LANES)))
        for ch in range(4)
    ]

    def look(idx):
        low = idx & (LANES - 1)
        high = idx >= LANES
        vals = []
        for lo_t, hi_t in tables:
            lo_v = jnp.take_along_axis(lo_t, low, axis=1, mode="promise_in_bounds")
            hi_v = jnp.take_along_axis(hi_t, low, axis=1, mode="promise_in_bounds")
            vals.append(jnp.where(high, hi_v, lo_v))
        return vals

    def group_body(g, carry):
        col = pl.ds(pl.multiple_of(g * LANES, LANES), LANES)
        col_l = pl.ds(pl.multiple_of(jnp.maximum(g - 1, 0) * LANES, LANES), LANES)
        col_r = pl.ds(pl.multiple_of(jnp.minimum(g + 1, groups - 1) * LANES, LANES), LANES)
        has_l = g > 0
        has_r = g < groups - 1
        centers = [[d_ref[p, pl.ds(k * 8, 8), col] for k in range(chunks)] for p in range(2)]
        for k in range(chunks):
            rows = pl.ds(k * 8, 8)
            samples = []
            for p in range(2):
                c = centers[p][k]
                if k == 0:
                    up_src = jnp.where(block == 0, htop_ref[p, :, col], dprev_ref[p, :, col])
                else:
                    up_src = centers[p][k - 1]
                if k == chunks - 1:
                    dn_src = jnp.where(block == last_block, hbot_ref[p, :, col], dnext_ref[p, :, col])
                else:
                    dn_src = centers[p][k + 1]
                up = jnp.where(sub == 0, pltpu.roll(up_src, 1, 0), pltpu.roll(c, 1, 0))
                dn = jnp.where(sub == 7, pltpu.roll(dn_src, 7, 0), pltpu.roll(c, 7, 0))
                grad_y = (dn - up) * 0.5
                left_src = jnp.where(has_l, d_ref[p, rows, col_l], 0.0)
                right_src = jnp.where(has_r, d_ref[p, rows, col_r], 0.0)
                lf = jnp.where(lane == 0, pltpu.roll(left_src, 1, 1), pltpu.roll(c, 1, 1))
                rt = jnp.where(lane == LANES - 1, pltpu.roll(right_src, LANES - 1, 1),
                               pltpu.roll(c, LANES - 1, 1))
                grad_z = (rt - lf) * 0.5
                if p == 0:
                    grad_x = (centers[1][k] - xp_ref[rows, col]) * 0.5
                else:
                    grad_x = (xn_ref[rows, col] - centers[0][k]) * 0.5
                lit = jnp.abs(0.48 * grad_x + 0.6 * grad_y + 0.64 * grad_z)
                shade = 0.3 + 0.7 * lit / jnp.sqrt(
                    grad_x * grad_x + grad_y * grad_y + grad_z * grad_z + 1.0)
                entries = look(b_ref[p, rows, col])
                optical = entries[3] * depth_scale
                absorb = 1.0 - jnp.exp(-optical)
                emitted = [entries[ch] * shade * absorb for ch in range(3)]
                samples.append((optical, emitted))
            (o0, e0), (o1, e1) = samples
            t0 = jnp.exp(-o0)
            for ch in range(3):
                out_ref[ch, rows, col] = e0[ch] + t0 * e1[ch]
            out_ref[3, rows, col] = jnp.exp(-(o0 + o1))
        return carry

    lax.fori_loop(0, groups, group_body, 0)


def render(density, bins, table, x_prev, x_next, h_top, h_bot, depth_scale):
    planes, rows, cols = density.shape
    n_blocks = rows // ROW_BLOCK
    eights = ROW_BLOCK // 8
    last8 = rows // 8 - 1
    blk3 = lambda r: (0, r, 0)
    return pl.pallas_call(
        functools.partial(render_kernel, depth_scale),
        grid=(n_blocks,),
        in_specs=[
            pl.BlockSpec((8, 2 * LANES), lambda r: (0, 0)),
            pl.BlockSpec((planes, ROW_BLOCK, cols), blk3),
            pl.BlockSpec((planes, 8, cols), lambda r: (0, jnp.maximum(r * eights - 1, 0), 0)),
            pl.BlockSpec((planes, 8, cols), lambda r: (0, jnp.minimum((r + 1) * eights, last8), 0)),
            pl.BlockSpec((planes, 8, cols), lambda r: (0, 0, 0)),
            pl.BlockSpec((planes, 8, cols), lambda r: (0, 0, 0)),
            pl.BlockSpec((ROW_BLOCK, cols), lambda r: (r, 0)),
            pl.BlockSpec((ROW_BLOCK, cols), lambda r: (r, 0)),
            pl.BlockSpec((planes, ROW_BLOCK, cols), blk3),
        ],
        out_specs=pl.BlockSpec((4, ROW_BLOCK, cols), blk3),
        out_shape=jax.ShapeDtypeStruct((4, rows, cols), jnp.float32),
    )(table, density, density, density, h_top, h_bot, x_prev, x_next, bins)


def per_device(density, bins, colors, extinction):
    depth_cells, row_cells, col_cells = density.shape
    slab_count = lax.axis_size("depth")
    tile_count = lax.axis_size("tile")
    depth_scale = 0.6 / (depth_cells * slab_count)
    fwd_d, bwd_d = shift_pair("depth", slab_count)
    fwd_t, bwd_t = shift_pair("tile", tile_count)
    x_prev = lax.ppermute(density[-1], "depth", fwd_d)
    x_next = lax.ppermute(density[0], "depth", bwd_d)
    h_top = lax.ppermute(density[:, row_cells - 8:], "tile", fwd_t)
    h_bot = lax.ppermute(density[:, :8], "tile", bwd_t)
    lookup = jnp.concatenate([colors, extinction[None, :]], 0).astype(jnp.float32)
    table = jnp.concatenate([lookup, jnp.zeros((4, lookup.shape[1]), jnp.float32)], 0)
    image_part = render(density, bins, table, x_prev, x_next, h_top, h_bot, depth_scale)
    slab_index = lax.axis_index("depth")
    for round_index in range(slab_count.bit_length() - 1):
        half_width = image_part.shape[2] // 2
        lower_part = image_part[:, :, :half_width]
        upper_part = image_part[:, :, half_width:]
        behind = jnp.right_shift(slab_index, round_index) % 2 == 1
        kept_part = jnp.where(behind, upper_part, lower_part)
        sent_part = jnp.where(behind, lower_part, upper_part)
        received = partner(sent_part, "depth", round_index)
        front = jnp.where(behind, received, kept_part)
        back = jnp.where(behind, kept_part, received)
        image_part = over_pair(front, back)
    return jnp.concatenate([image_part[:3], 1.0 - image_part[3:]], 0)


def solution(mesh):
    return jax.shard_map(
        per_device,
        mesh=mesh,
        in_specs=(P("depth", "tile", None), P("depth", "tile", None), P(), P()),
        out_specs=P(None, "tile", "depth"),
        check_vma=False,
    )
```

time: 222 us -> 139 us (0.63)
  other arithmetic: 51.7 us -> 10.9 us
  local copies, waits for them, and re-layouts: 46.7 us -> 6.3 us
  matrix products: 39.6 us -> 0 us
  waiting for transfers between devices: 52.7 us -> 75.5 us
  Pallas kernels: 0 us -> 16.5 us
    dot_general x16 -> x0, matrix products: 39.6 us -> none  [look_block(): jnp.dot(table_rows, onehot_low, preferred_element_type=jnp.float32)]
    slice x4 -> x1, local copies, waits for them, and re-layouts: 20.1 us -> 1.63 us  [per_device(): h_bot = lax.ppermute(density[:, :8], 'tile', bwd_t)]
    ppermute x6, waiting for transfers between devices: 52.7 us -> 70.2 us  [partner(): lax.ppermute(value, axis, [(i, i ^ 1 << stride) for i in range(lax.axis_s...]
    pallas_call x0 -> x1, Pallas kernels: none -> 16.5 us  [render(): pl.pallas_call(functools.partial(render_kernel, depth_scale), grid=(n_blo...]
    select_n x32 -> x0, other arithmetic: 16 us -> none  [the longest x16 8.83 us: look_block(): high_digit = bin_block // low_count]
    dynamic_update_slice x16 -> x0, local copies, waits for them, and re-layouts: 13.5 us -> none  [per_device(): entries = lax.map(look_block, bins.reshape(-1, block_size))]
    mul x1 -> x0, other arithmetic: 10.2 us -> none  [per_device(): optical = entries[3] * depth_scale]
    reduce_sum x1 -> x0, other arithmetic: 5.89 us -> none  [per_device(): radiance = jnp.sum(jnp.exp(-(running - optical)) * emitted, axis=1)]
  transfers between devices with their start and end apart: 10 -> 10, of which waited for: 6 -> 9; matrix products, arithmetic and copies ran while one was open for 52% -> 2% of each run, Pallas kernels for 0% -> 0%
where the time goes in v1:
time: 139 us; the launch traced here: 137 us
  waiting for transfers between devices  75.5 us (54%)
  starting transfers between devices  27.4 us (20%)
  Pallas kernels  16.5 us (12%)
  other arithmetic  10.9 us (8%)
  local copies, waits for them, and re-layouts  6.3 us (5%)
    ppermute x6, waiting for transfers between devices, partner(): lax.ppermute(value, axis, [(i, i ^ 1 << stride) for i in range(lax.axis_s...  70.2 us
    ppermute x6, starting transfers between devices, partner(): lax.ppermute(value, axis, [(i, i ^ 1 << stride) for i in range(lax.axis_s...  17.2 us
    pallas_call x1, Pallas kernels, render(): pl.pallas_call(functools.partial(render_kernel, depth_scale), grid=(n_blo...  16.5 us
    select_n x6, other arithmetic, per_device(): front = jnp.where(behind, received, kept_part)  5.58 us
    ppermute x1, waiting for transfers between devices, per_device(): h_bot = lax.ppermute(density[:, :8], 'tile', bwd_t)  3.8 us
    ppermute x1, starting transfers between devices, per_device(): x_next = lax.ppermute(density[0], 'depth', bwd_d)  3.64 us
    ppermute x1, starting transfers between devices, per_device(): h_top = lax.ppermute(density[:, row_cells - 8:], 'tile', fwd_t)  3.39 us
    select_n x6, other arithmetic, per_device(): sent_part = jnp.where(behind, lower_part, upper_part)  3.18 us
  transfers between devices with their start and end apart: 10, of which 9 were waited for; matrix products, arithmetic and copies ran while one was open for 2% of the time, Pallas kernels for 0%

profile of v1, /device:TPU:8, one launch (start us, length us, event | category | flops | bytes accessed | tf_op | source)
XLA Modules:
  0.0 136.9 jit_solution(2125735308907545942)
XLA Ops:
  0.0 0.0 copy-start.5
  0.0 2.7 %slice_bitcast_fusion = (f32[128,2048]{1,0:T(8,128)S(1)}, f32[128,2048]{1,0:T(8,128)}) fusion(f32[2,128,2048]{2,1,0:T(8,128)} %dnext_ref.1), kind=kLoop, calls=%fused_computation.10 | loop fusion | bytes 4194304 | tf_op jit(solution)/shard_map/squeeze | solution.py:134
  2.8 1.9 %collective-permute-start.2 = (f32[128,2048]{1,0:T(8,128)}, f32[128,2048]{1,0:T(8,128)S(1)}, u32[]{:S(2)}, u32[]{:S(2)}) collective-permute-start(f32[128,2048]{1,0:T(8,128)} %get-tuple-element.12), channel_id=1, source_target_pairs={{0,4},{4,8},{8,12},{12,16},{16,20},{20,24},{24,28},{28,32},{32,36}... | collective-permute-start | bytes 3145736 | tf_op jit(solution)/shard_map/ppermute | solution.py:133
  4.7 3.6 %collective-permute-start.3 = (f32[128,2048]{1,0:T(8,128)S(1)}, f32[128,2048]{1,0:T(8,128)S(1)}, u32[]{:S(2)}, u32[]{:S(2)}) collective-permute-start(f32[128,2048]{1,0:T(8,128)S(1)} %get-tuple-element.11), channel_id=1, source_target_pairs={{4,0},{8,4},{12,8},{16,12},{20,16},{24,20},{28,24},{32,28},{36,32}... | collective-permute-start | bytes 3145736 | tf_op jit(solution)/shard_map/ppermute | solution.py:134
  8.3 1.6 %fusion.18 = (f32[2,8,2048]{2,1,0:T(8,128)S(1)}, f32[2,8,2048]{2,1,0:T(8,128)}) fusion(f32[2,128,2048]{2,1,0:T(8,128)} %dnext_ref.1), kind=kLoop, calls=%fused_computation.73 | loop fusion | bytes 524288 | tf_op jit(solution)/shard_map/slice | solution.py:136
  9.9 3.4 %collective-permute-start = (f32[2,8,2048]{2,1,0:T(8,128)}, f32[2,8,2048]{2,1,0:T(8,128)S(1)}, u32[]{:S(2)}, u32[]{:S(2)}) collective-permute-start(f32[2,8,2048]{2,1,0:T(8,128)} %get-tuple-element.14), channel_id=1, source_target_pairs={{0,1},{1,2},{2,3},{4,5},{5,6},{6,7},{8,9},{9,10},{10,11},{12,13},{... | collective-permute-start | bytes 393224 | tf_op jit(solution)/shard_map/ppermute | solution.py:135
  13.3 1.3 collective-permute-start.1
  14.7 0.0 copy-done.5
  14.7 0.0 copy-done.4
  14.7 0.6 fusion.17.table_ref
  15.3 1.2 collective-permute-done.htop_ref
  16.5 3.8 %collective-permute-done.1.hbot_ref = f32[2,8,2048]{2,1,0:T(8,128)S(1)} collective-permute-done((f32[2,8,2048]{2,1,0:T(8,128)S(1)}, f32[2,8,2048]{2,1,0:T(8,128)S(1)}, u32[]{:S(2)}, u32[]{:S(2)}) %collective-permute-start.1) | collective-permute-done | bytes 131104 | tf_op jit(solution)/shard_map/ppermute | solution.py:136
  20.3 0.0 collective-permute-done.2.xp_ref
  20.3 0.3 collective-permute-done.3.xn_ref
  20.6 0.0 copy-done.2
  20.6 0.4 copy-done.3
  21.0 0.4 copy-done
  21.4 1.0 copy-done.1
  22.4 16.5 %shard_map.46 = f32[4,128,2048]{2,1,0:T(8,128)} custom-call(f32[8,256]{1,0:T(8,128)} %fusion.17.table_ref, f32[2,128,2048]{2,1,0:T(8,128)} %dnext_ref.1, f32[2,128,2048]{2,1,0:T(8,128)} %dnext_ref.1, f32[2,128,2048]{2,1,0:T(8,128)} %dnext_ref.1, f32[2,8,2048]{2,1,0:T(8,128)} %copy-done.2, f32[2,8,2048]{2,1,0:T(8,128)} %copy-done.3, f32[128,2048]{1,0:T(8,128)} %copy-done, ...), custom_call_target="tpu_custom_call" | custom-call | tf_op jit(solution)/shard_map/pallas_call | solution.py:107
  38.9 2.6 %slice_select_fusion.1 = f32[4,128,1024]{2,1,0:T(8,128)S(1)} fusion(f32[4,128,2048]{2,1,0:T(8,128)} %shard_map.46, pred[]{:T(512)S(6)} %eq.30), kind=kLoop, calls=%fused_computation.3 | loop fusion | flops 524288 | bytes 6291457 | tf_op jit(solution)/shard_map/jit(_where)/select_n | solution.py:147
  41.5 1.2 collective-permute-start.4
  42.7 3.9 %collective-permute-done.4 = f32[4,128,1024]{2,1,0:T(8,128)} collective-permute-done((f32[4,128,1024]{2,1,0:T(8,128)S(1)}, f32[4,128,1024]{2,1,0:T(8,128)}, u32[]{:S(2)}, u32[]{:S(2)}) %collective-permute-start.4) | collective-permute-done | bytes 2097184 | tf_op jit(solution)/shard_map/ppermute | solution.py:19
  46.6 3.6 %broadcast_select_fusion.1 = (f32[4,128,1024]{2,1,0:T(8,128)S(1)}, f32[4,128,1024]{2,1,0:T(8,128)S(1)}) fusion(f32[4,128,1024]{2,1,0:T(8,128)} %collective-permute-done.4, pred[]{:T(512)S(6)} %eq.30, f32[4,128,2048]{2,1,0:T(8,128)} %shard_map.46), kind=kLoop, calls=%fused_computation.13 | loop fusion | flops 1572864 | bytes 10485761 | tf_op jit(solution)/shard_map/jit(_where)/select_n | solution.py:149
  50.2 0.1 slice_bitcast_fusion.2
  50.3 0.4 fusion
  50.6 0.2 broadcast_select_fusion.5
  50.9 0.6 collective-permute-start.5
  51.4 25.1 %collective-permute-done.5 = f32[4,128,512]{2,1,0:T(8,128)} collective-permute-done((f32[4,128,512]{2,1,0:T(8,128)S(1)}, f32[4,128,512]{2,1,0:T(8,128)}, u32[]{:S(2)}, u32[]{:S(2)}) %collective-permute-start.5) | collective-permute-done | bytes 1048608 | tf_op jit(solution)/shard_map/ppermute | solution.py:19
  76.5 1.6 %broadcast_select_fusion.3 = (f32[4,128,512]{2,1,0:T(8,128)S(1)}, f32[4,128,512]{2,1,0:T(8,128)S(1)}) fusion(f32[4,128,512]{2,1,0:T(8,128)} %collective-permute-done.5, pred[]{:T(512)S(6)} %eq.29, f32[1,128,1024]{2,1,0:T(8,128)S(1)} %get-tuple-element.10, f32[3,128,1024]{2,1,0:T(8,128)S(1)} %fusion), kind=kLoop, calls=%fused_computation.22 | loop fusion | flops 1835008 | bytes 5242881 | tf_op jit(solution)/shard_map/jit(_where)/select_n | solution.py:149
  78.1 0.2 fusion.2
  78.3 0.1 broadcast_select_fusion.9
  78.4 4.5 %collective-permute-start.6 = (f32[4,128,256]{2,1,0:T(8,128)S(1)}, f32[4,128,256]{2,1,0:T(8,128)S(1)}, u32[]{:S(2)}, u32[]{:S(2)}) collective-permute-start(f32[4,128,256]{2,1,0:T(8,128)S(1)} %broadcast_select_fusion.9), channel_id=1, source_target_pairs={{0,16},{4,20},{8,24},{12,28},{16,0},{20,4},{24,8},{28,12},{32,48},... | collective-permute-start | bytes 1572872 | tf_op jit(solution)/shard_map/ppermute | solution.py:19
  82.9 11.6 %collective-permute-done.6 = f32[4,128,256]{2,1,0:T(8,128)S(1)} collective-permute-done((f32[4,128,256]{2,1,0:T(8,128)S(1)}, f32[4,128,256]{2,1,0:T(8,128)S(1)}, u32[]{:S(2)}, u32[]{:S(2)}) %collective-permute-start.6) | collective-permute-done | bytes 524320 | tf_op jit(solution)/shard_map/ppermute | solution.py:19
  94.5 0.1 broadcast_select_fusion.7
  94.7 0.1 fusion.4
  94.8 2.0 %collective-permute-start.7 = (f32[4,128,128]{2,1,0:T(8,128)S(1)}, f32[4,128,128]{2,1,0:T(8,128)S(1)}, u32[]{:S(2)}, u32[]{:S(2)}) collective-permute-start(f32[4,128,128]{2,1,0:T(8,128)S(1)} %broadcast_select_fusion.13), channel_id=1, source_target_pairs={{0,32},{4,36},{8,40},{12,44},{16,48},{20,52},{24,56},{28,60},{32,0... | collective-permute-start | bytes 786440 | tf_op jit(solution)/shard_map/ppermute | solution.py:19
  96.8 5.4 %collective-permute-done.7 = f32[4,128,128]{2,1,0:T(8,128)S(1)} collective-permute-done((f32[4,128,128]{2,1,0:T(8,128)S(1)}, f32[4,128,128]{2,1,0:T(8,128)S(1)}, u32[]{:S(2)}, u32[]{:S(2)}) %collective-permute-start.7) | collective-permute-done | bytes 262176 | tf_op jit(solution)/shard_map/ppermute | solution.py:19
  102.3 0.1 fusion.6
  102.5 5.8 %collective-permute-start.8 = (f32[4,128,64]{2,1,0:T(8,128)S(1)}, f32[4,128,64]{2,1,0:T(8,128)S(1)}, u32[]{:S(2)}, u32[]{:S(2)}) collective-permute-start(f32[4,128,64]{2,1,0:T(8,128)S(1)} %fusion.6), channel_id=1, source_target_pairs={{0,64},{4,68},{8,72},{12,76},{16,80},{20,84},{24,88},{28,92},{32,9... | collective-permute-start | bytes 393224 | tf_op jit(solution)/shard_map/ppermute | solution.py:19
  108.2 10.4 %collective-permute-done.8 = f32[4,128,64]{2,1,0:T(8,128)S(1)} collective-permute-done((f32[4,128,64]{2,1,0:T(8,128)S(1)}, f32[4,128,64]{2,1,0:T(8,128)S(1)}, u32[]{:S(2)}, u32[]{:S(2)}) %collective-permute-start.8) | collective-permute-done | bytes 131104 | tf_op jit(solution)/shard_map/ppermute | solution.py:19
  118.7 0.1 broadcast_select_fusion.15
  118.8 0.1 fusion.8
  119.0 3.2 %collective-permute-start.9 = (f32[4,128,32]{2,1,0:T(8,128)S(1)}, f32[4,128,32]{2,1,0:T(8,128)S(1)}, u32[]{:S(2)}, u32[]{:S(2)}) collective-permute-start(f32[4,128,32]{2,1,0:T(8,128)S(1)} %fusion.8), channel_id=1, source_target_pairs={{0,128},{4,132},{8,136},{12,140},{16,144},{20,148},{24,152},{28,15... | collective-permute-start | bytes 196616 | tf_op jit(solution)/shard_map/ppermute | solution.py:19
  122.2 13.7 %collective-permute-done.9 = f32[4,128,32]{2,1,0:T(8,128)S(1)} collective-permute-done((f32[4,128,32]{2,1,0:T(8,128)S(1)}, f32[4,128,32]{2,1,0:T(8,128)S(1)}, u32[]{:S(2)}, u32[]{:S(2)}) %collective-permute-start.9) | collective-permute-done | bytes 65568 | tf_op jit(solution)/shard_map/ppermute | solution.py:19
  135.9 0.1 broadcast_select_fusion.17
  136.1 0.1 copy.9
  136.2 0.1 copy.10
  136.2 0.7 pad_maximum_fusion.5
  (16 shorter events, 0.3 us)
Async XLA Ops:
  0.0 14.7 %copy-start.5 = (bf16[256]{0:T(256)(128)(2,1)S(1)}, bf16[256]{0:T(256)(128)(2,1)}, u32[]{:S(2)}) copy-start(bf16[256]{0:T(256)(128)(2,1)} %param.7) | copy-start | bytes 1540
  0.0 14.7 %copy-start.4 = (bf16[3,256]{1,0:T(4,128)(2,1)S(1)}, bf16[3,256]{1,0:T(4,128)(2,1)}, u32[]{:S(2)}) copy-start(bf16[3,256]{1,0:T(4,128)(2,1)} %param.6) | copy-start | bytes 4612
  2.8 17.6 %collective-permute-start.2 = (f32[128,2048]{1,0:T(8,128)}, f32[128,2048]{1,0:T(8,128)S(1)}, u32[]{:S(2)}, u32[]{:S(2)}) collective-permute-start(f32[128,2048]{1,0:T(8,128)} %get-tuple-element.12), channel_id=1, source_target_pairs={{0,4},{4,8},{8,12},{12,16},{16,20},{20,24},{24,28},{28,32},{32,36}... | collective-permute-start | bytes 3145736 | tf_op jit(solution)/shard_map/ppermute | solution.py:133
  4.7 15.9 %collective-permute-start.3 = (f32[128,2048]{1,0:T(8,128)S(1)}, f32[128,2048]{1,0:T(8,128)S(1)}, u32[]{:S(2)}, u32[]{:S(2)}) collective-permute-start(f32[128,2048]{1,0:T(8,128)S(1)} %get-tuple-element.11), channel_id=1, source_target_pairs={{4,0},{8,4},{12,8},{16,12},{20,16},{24,20},{28,24},{32,28},{36,32}... | collective-permute-start | bytes 3145736 | tf_op jit(solution)/shard_map/ppermute | solution.py:134
  9.9 6.6 %collective-permute-start = (f32[2,8,2048]{2,1,0:T(8,128)}, f32[2,8,2048]{2,1,0:T(8,128)S(1)}, u32[]{:S(2)}, u32[]{:S(2)}) collective-permute-start(f32[2,8,2048]{2,1,0:T(8,128)} %get-tuple-element.14), channel_id=1, source_target_pairs={{0,1},{1,2},{2,3},{4,5},{5,6},{6,7},{8,9},{9,10},{10,11},{12,13},{... | collective-permute-start | bytes 393224 | tf_op jit(solution)/shard_map/ppermute | solution.py:135
  13.3 7.0 %collective-permute-start.1 = (f32[2,8,2048]{2,1,0:T(8,128)S(1)}, f32[2,8,2048]{2,1,0:T(8,128)S(1)}, u32[]{:S(2)}, u32[]{:S(2)}) collective-permute-start(f32[2,8,2048]{2,1,0:T(8,128)S(1)} %get-tuple-element.13), channel_id=1, source_target_pairs={{1,0},{2,1},{3,2},{5,4},{6,5},{7,6},{9,8},{10,9},{11,10},{13,12},{... | collective-permute-start | bytes 393224 | tf_op jit(solution)/shard_map/ppermute | solution.py:136
  16.5 4.1 %copy-start.2 = (f32[2,8,2048]{2,1,0:T(8,128)}, f32[2,8,2048]{2,1,0:T(8,128)S(1)}, u32[]{:S(2)}) copy-start(f32[2,8,2048]{2,1,0:T(8,128)S(1)} %collective-permute-done.htop_ref) | copy-start | bytes 393220
  20.3 0.7 copy-start.3
  20.3 1.1 copy-start
  21.4 1.0 copy-start.1
  41.5 5.1 %collective-permute-start.4 = (f32[4,128,1024]{2,1,0:T(8,128)S(1)}, f32[4,128,1024]{2,1,0:T(8,128)}, u32[]{:S(2)}, u32[]{:S(2)}) collective-permute-start(f32[4,128,1024]{2,1,0:T(8,128)S(1)} %slice_select_fusion.1), channel_id=1, source_target_pairs={{0,4},{4,0},{8,12},{12,8},{16,20},{20,16},{24,28},{28,24},{32,36},... | collective-permute-start | bytes 6291464 | tf_op jit(solution)/shard_map/ppermute | solution.py:19
  50.9 25.6 %collective-permute-start.5 = (f32[4,128,512]{2,1,0:T(8,128)S(1)}, f32[4,128,512]{2,1,0:T(8,128)}, u32[]{:S(2)}, u32[]{:S(2)}) collective-permute-start(f32[4,128,512]{2,1,0:T(8,128)S(1)} %broadcast_select_fusion.5), channel_id=1, source_target_pairs={{0,8},{4,12},{8,0},{12,4},{16,24},{20,28},{24,16},{28,20},{32,40},... | collective-permute-start | bytes 3145736 | tf_op jit(solution)/shard_map/ppermute | solution.py:19
  78.4 16.1 %collective-permute-start.6 = (f32[4,128,256]{2,1,0:T(8,128)S(1)}, f32[4,128,256]{2,1,0:T(8,128)S(1)}, u32[]{:S(2)}, u32[]{:S(2)}) collective-permute-start(f32[4,128,256]{2,1,0:T(8,128)S(1)} %broadcast_select_fusion.9), channel_id=1, source_target_pairs={{0,16},{4,20},{8,24},{12,28},{16,0},{20,4},{24,8},{28,12},{32,48},... | collective-permute-start | bytes 1572872 | tf_op jit(solution)/shard_map/ppermute | solution.py:19
  94.8 7.4 %collective-permute-start.7 = (f32[4,128,128]{2,1,0:T(8,128)S(1)}, f32[4,128,128]{2,1,0:T(8,128)S(1)}, u32[]{:S(2)}, u32[]{:S(2)}) collective-permute-start(f32[4,128,128]{2,1,0:T(8,128)S(1)} %broadcast_select_fusion.13), channel_id=1, source_target_pairs={{0,32},{4,36},{8,40},{12,44},{16,48},{20,52},{24,56},{28,60},{32,0... | collective-permute-start | bytes 786440 | tf_op jit(solution)/shard_map/ppermute | solution.py:19
  102.5 16.2 %collective-permute-start.8 = (f32[4,128,64]{2,1,0:T(8,128)S(1)}, f32[4,128,64]{2,1,0:T(8,128)S(1)}, u32[]{:S(2)}, u32[]{:S(2)}) collective-permute-start(f32[4,128,64]{2,1,0:T(8,128)S(1)} %fusion.6), channel_id=1, source_target_pairs={{0,64},{4,68},{8,72},{12,76},{16,80},{20,84},{24,88},{28,92},{32,9... | collective-permute-start | bytes 393224 | tf_op jit(solution)/shard_map/ppermute | solution.py:19
  119.0 16.9 %collective-permute-start.9 = (f32[4,128,32]{2,1,0:T(8,128)S(1)}, f32[4,128,32]{2,1,0:T(8,128)S(1)}, u32[]{:S(2)}, u32[]{:S(2)}) collective-permute-start(f32[4,128,32]{2,1,0:T(8,128)S(1)} %fusion.8), channel_id=1, source_target_pairs={{0,128},{4,132},{8,136},{12,140},{16,144},{20,148},{24,152},{28,15... | collective-permute-start | bytes 196616 | tf_op jit(solution)/shard_map/ppermute | solution.py:19

commit v2 on v1

--- a/solution.py
+++ b/solution.py
@@ -123,6 +123,113 @@
     )(table, density, density, density, h_top, h_bot, x_prev, x_next, bins)
 
 
+def combine_into(dst_ref, kept_ref, kept_off, rcv_ref, behind, rows, width, lane_axis, finish=False):
+    chunk_rows = 8
+    lanes = min(width, LANES) if lane_axis else LANES
+    groups = width // lanes if lane_axis else 1
+
+    def body(i, carry):
+        for j in range(groups):
+            if lane_axis:
+                r_sl = pl.ds(pl.multiple_of(i * chunk_rows, chunk_rows), chunk_rows)
+                k_sl = (r_sl, pl.ds(pl.multiple_of(kept_off + j * lanes, lanes), lanes))
+                d_sl = (r_sl, pl.ds(j * lanes, lanes))
+            else:
+                r_k = pl.ds(pl.multiple_of(kept_off + i * chunk_rows, chunk_rows), chunk_rows)
+                r_d = pl.ds(pl.multiple_of(i * chunk_rows, chunk_rows), chunk_rows)
+                k_sl = (r_k, slice(None))
+                d_sl = (r_d, slice(None))
+            kept = [kept_ref[(ch,) + k_sl] for ch in range(4)]
+            rcv = [rcv_ref[(ch,) + d_sl] for ch in range(4)]
+            front = [jnp.where(behind, b, a) for a, b in zip(kept, rcv)]
+            back = [jnp.where(behind, a, b) for a, b in zip(kept, rcv)]
+            for ch in range(3):
+                dst_ref[(ch,) + d_sl] = front[ch] + front[3] * back[ch]
+            trans = front[3] * back[3]
+            dst_ref[(3,) + d_sl] = (1.0 - trans) if finish else trans
+        return carry
+
+    lax.fori_loop(0, rows // chunk_rows, body, 0)
+
+
+def composite_kernel(n_rounds, lane_rounds, img_ref, out_ref, *scratch):
+    recv = scratch[:n_rounds]
+    acc = scratch[n_rounds:2 * n_rounds - 1]
+    flip_ref = scratch[2 * n_rounds - 1]
+    send_sems, recv_sems = scratch[2 * n_rounds:]
+    me = lax.axis_index("depth")
+    tile = lax.axis_index("tile")
+    bits = [(me // (1 << r)) % 2 for r in range(n_rounds)]
+    partners = [me + (1 - 2 * bits[r]) * (1 << r) for r in range(n_rounds)]
+
+    barrier = pltpu.get_barrier_semaphore()
+    for r in range(n_rounds):
+        pl.semaphore_signal(barrier, inc=1, device_id=(partners[r], tile),
+                            device_id_type=pl.DeviceIdType.MESH)
+    pl.semaphore_wait(barrier, n_rounds)
+
+    rows = img_ref.shape[1]
+    width = img_ref.shape[2]
+    src = img_ref
+    for r in range(n_rounds):
+        half = width >> (r + 1)
+        behind = bits[r] == 1
+        send_off = (1 - bits[r]) * half
+        keep_off = bits[r] * half
+        lane_axis = r < lane_rounds
+        if r == lane_rounds:
+            for ch in range(4):
+                flip_ref[ch] = src[ch].T
+            src = flip_ref
+        if lane_axis:
+            src_view = src.at[:, :, pl.ds(pl.multiple_of(send_off, LANES), half)]
+        else:
+            src_view = src.at[:, pl.ds(pl.multiple_of(send_off, 8), half), :]
+        copy = pltpu.make_async_remote_copy(
+            src_ref=src_view,
+            dst_ref=recv[r],
+            send_sem=send_sems.at[r],
+            recv_sem=recv_sems.at[r],
+            device_id=(partners[r], tile),
+            device_id_type=pl.DeviceIdType.MESH,
+        )
+        copy.start()
+        copy.wait()
+        last = r == n_rounds - 1
+        dst = out_ref if last else acc[r]
+        if lane_axis:
+            combine_into(dst, src, keep_off, recv[r], behind, rows, half, True)
+        else:
+            combine_into(dst, src, keep_off, recv[r], behind, half, rows, False, finish=last)
+        src = dst
+
+
+def composite(image_part, n_rounds):
+    chans, rows, width = image_part.shape
+    lane_rounds = 0
+    while (width >> (lane_rounds + 1)) >= LANES and lane_rounds < n_rounds:
+        lane_rounds += 1
+    recv_shapes = []
+    for r in range(n_rounds):
+        half = width >> (r + 1)
+        recv_shapes.append((chans, rows, half) if r < lane_rounds else (chans, half, rows))
+    final = recv_shapes[-1]
+    scratch = [pltpu.VMEM(s, jnp.float32) for s in recv_shapes]
+    scratch += [pltpu.VMEM(s, jnp.float32) for s in recv_shapes[:-1]]
+    scratch += [pltpu.VMEM((chans, width >> lane_rounds, rows), jnp.float32)]
+    scratch += [pltpu.SemaphoreType.DMA((n_rounds,)), pltpu.SemaphoreType.DMA((n_rounds,))]
+    out = pl.pallas_call(
+        functools.partial(composite_kernel, n_rounds, lane_rounds),
+        out_shape=jax.ShapeDtypeStruct(final, jnp.float32),
+        in_specs=[pl.BlockSpec(memory_space=pltpu.VMEM)],
+        out_specs=pl.BlockSpec(memory_space=pltpu.VMEM),
+        scratch_shapes=scratch,
+        compiler_params=pltpu.CompilerParams(
+            collective_id=0, has_side_effects=True, vmem_limit_bytes=48 * 1024 * 1024),
+    )(image_part)
+    return jnp.transpose(out, (0, 2, 1))
+
+
 def per_device(density, bins, colors, extinction):
     depth_cells, row_cells, col_cells = density.shape
     slab_count = lax.axis_size("depth")
@@ -137,19 +244,7 @@
     lookup = jnp.concatenate([colors, extinction[None, :]], 0).astype(jnp.float32)
     table = jnp.concatenate([lookup, jnp.zeros((4, lookup.shape[1]), jnp.float32)], 0)
     image_part = render(density, bins, table, x_prev, x_next, h_top, h_bot, depth_scale)
-    slab_index = lax.axis_index("depth")
-    for round_index in range(slab_count.bit_length() - 1):
-        half_width = image_part.shape[2] // 2
-        lower_part = image_part[:, :, :half_width]
-        upper_part = image_part[:, :, half_width:]
-        behind = jnp.right_shift(slab_index, round_index) % 2 == 1
-        kept_part = jnp.where(behind, upper_part, lower_part)
-        sent_part = jnp.where(behind, lower_part, upper_part)
-        received = partner(sent_part, "depth", round_index)
-        front = jnp.where(behind, received, kept_part)
-        back = jnp.where(behind, kept_part, received)
-        image_part = over_pair(front, back)
-    return jnp.concatenate([image_part[:3], 1.0 - image_part[3:]], 0)
+    return composite(image_part, slab_count.bit_length() - 1)
 
 
 def solution(mesh):

time: 139 us -> 113 us (0.81); the launches traced: 137 us -> 113 us
  Pallas kernels: 16.5 us -> 88.4 us
  waiting for transfers between devices: 75.5 us -> 6.76 us
  starting transfers between devices: 27.4 us -> 10.2 us
  other arithmetic: 10.9 us -> 0.61 us
    pallas_call x0 -> x1, Pallas kernels: none -> 71.9 us  [composite(): pl.pallas_call(functools.partial(composite_kernel, n_rounds, lane_rounds)...]
    ppermute x6 -> x0, waiting for transfers between devices: 70.2 us -> none  [partner(): lax.ppermute(value, axis, [(i, i ^ 1 << stride) for i in range(lax.axis_s...]
    ppermute x6 -> x0, starting transfers between devices: 17.2 us -> none  [partner(): lax.ppermute(value, axis, [(i, i ^ 1 << stride) for i in range(lax.axis_s...]
    select_n x12 -> x0, other arithmetic: 8.77 us -> none  [the longest x6 5.58 us: per_device(): front = jnp.where(behind, received, kept_part)]
    ppermute x1, waiting for transfers between devices: 0.01 us -> 3.57 us  [per_device(): x_prev = lax.ppermute(density[-1], 'depth', fwd_d)]
    ppermute x1, waiting for transfers between devices: 3.8 us -> 1.54 us  [per_device(): h_bot = lax.ppermute(density[:, :8], 'tile', bwd_t)]
    unnamed x12 -> x15, local copies, waits for them, and re-layouts: 1.77 us -> 3.8 us
    ppermute x1, starting transfers between devices: 3.64 us -> 1.92 us  [per_device(): x_next = lax.ppermute(density[0], 'depth', bwd_d)]
  transfers between devices with their start and end apart: 10 -> 4, of which waited for: 9 -> 3; matrix products, arithmetic and copies ran while one was open for 2% -> 1% of each run, Pallas kernels for 0% -> 0%
where the time goes in v2:
time: 113 us
  Pallas kernels  88.4 us (78%)
  starting transfers between devices  10.2 us (9%)
  waiting for transfers between devices  6.76 us (6%)
  local copies, waits for them, and re-layouts  6.49 us (6%)
    pallas_call x1, Pallas kernels, composite(): pl.pallas_call(functools.partial(composite_kernel, n_rounds, lane_rounds)...  71.9 us
    pallas_call x1, Pallas kernels, render(): pl.pallas_call(functools.partial(render_kernel, depth_scale), grid=(n_blo...  16.5 us
    ppermute x1, starting transfers between devices, per_device(): h_top = lax.ppermute(density[:, row_cells - 8:], 'tile', fwd_t)  4.55 us
    unnamed x15, local copies, waits for them, and re-layouts  3.8 us
    ppermute x1, waiting for transfers between devices, per_device(): x_prev = lax.ppermute(density[-1], 'depth', fwd_d)  3.57 us
    ppermute x1, starting transfers between devices, per_device(): x_prev = lax.ppermute(density[-1], 'depth', fwd_d)  2.41 us
  transfers between devices with their start and end apart: 4, of which 3 were waited for; matrix products, arithmetic and copies ran while one was open for 1% of the time, Pallas kernels for 0%

profile of v2, /device:TPU:8, one launch (start us, length us, event | category | flops | bytes accessed | tf_op | source)
XLA Modules:
  0.0 112.5 jit_solution(11075668064760613947)
XLA Ops:
  0.0 0.0 copy-start.6
  0.0 0.0 copy-start.5
  0.0 1.7 %slice_bitcast_fusion = (f32[128,2048]{1,0:T(8,128)S(1)}, f32[128,2048]{1,0:T(8,128)S(1)}) fusion(f32[2,128,2048]{2,1,0:T(8,128)} %dnext_ref.1), kind=kLoop, calls=%fused_computation | loop fusion | bytes 4194304 | tf_op jit(solution)/shard_map/squeeze | solution.py:241
  1.7 1.9 %collective-permute-start.3 = (f32[128,2048]{1,0:T(8,128)S(1)}, f32[128,2048]{1,0:T(8,128)S(1)}, u32[]{:S(2)}, u32[]{:S(2)}) collective-permute-start(f32[128,2048]{1,0:T(8,128)S(1)} %get-tuple-element.5), channel_id=1, source_target_pairs={{4,0},{8,4},{12,8},{16,12},{20,16},{24,20},{28,24},{32,28},{36,32}... | collective-permute-start | bytes 3145736 | tf_op jit(solution)/shard_map/ppermute | solution.py:241
  3.6 2.4 %collective-permute-start.2 = (f32[128,2048]{1,0:T(8,128)S(1)}, f32[128,2048]{1,0:T(8,128)S(1)}, u32[]{:S(2)}, u32[]{:S(2)}) collective-permute-start(f32[128,2048]{1,0:T(8,128)S(1)} %get-tuple-element.6), channel_id=1, source_target_pairs={{0,4},{4,8},{8,12},{12,16},{16,20},{20,24},{24,28},{28,32},{32,36}... | collective-permute-start | bytes 3145736 | tf_op jit(solution)/shard_map/ppermute | solution.py:240
  6.1 1.0 fusion.4
  7.1 1.3 %collective-permute-start.1 = (f32[2,8,2048]{2,1,0:T(8,128)S(1)}, f32[2,8,2048]{2,1,0:T(8,128)S(1)}, u32[]{:S(2)}, u32[]{:S(2)}) collective-permute-start(f32[2,8,2048]{2,1,0:T(8,128)S(1)} %get-tuple-element.7), channel_id=1, source_target_pairs={{1,0},{2,1},{3,2},{5,4},{6,5},{7,6},{9,8},{10,9},{11,10},{13,12},{... | collective-permute-start | bytes 393224 | tf_op jit(solution)/shard_map/ppermute | solution.py:243
  8.4 4.6 %collective-permute-start = (f32[2,8,2048]{2,1,0:T(8,128)S(1)}, f32[2,8,2048]{2,1,0:T(8,128)S(1)}, u32[]{:S(2)}, u32[]{:S(2)}) collective-permute-start(f32[2,8,2048]{2,1,0:T(8,128)S(1)} %get-tuple-element.8), channel_id=1, source_target_pairs={{0,1},{1,2},{2,3},{4,5},{5,6},{6,7},{8,9},{9,10},{10,11},{12,13},{... | collective-permute-start | bytes 393224 | tf_op jit(solution)/shard_map/ppermute | solution.py:242
  12.9 0.0 copy-done.6
  12.9 0.0 copy-done.5
  12.9 0.6 fusion.3.table_ref
  13.6 1.5 %collective-permute-done.1.hbot_ref = f32[2,8,2048]{2,1,0:T(8,128)S(1)} collective-permute-done((f32[2,8,2048]{2,1,0:T(8,128)S(1)}, f32[2,8,2048]{2,1,0:T(8,128)S(1)}, u32[]{:S(2)}, u32[]{:S(2)}) %collective-permute-start.1) | collective-permute-done | bytes 131104 | tf_op jit(solution)/shard_map/ppermute | solution.py:243
  15.1 0.0 copy-start.3
  15.1 1.6 %collective-permute-done.htop_ref = f32[2,8,2048]{2,1,0:T(8,128)S(1)} collective-permute-done((f32[2,8,2048]{2,1,0:T(8,128)S(1)}, f32[2,8,2048]{2,1,0:T(8,128)S(1)}, u32[]{:S(2)}, u32[]{:S(2)}) %collective-permute-start) | collective-permute-done | bytes 131104 | tf_op jit(solution)/shard_map/ppermute | solution.py:242
  16.7 0.0 copy-start.4
  16.7 0.0 collective-permute-done.3.xn_ref
  16.8 0.0 copy-start.1
  16.8 3.6 %collective-permute-done.2.xp_ref = f32[128,2048]{1,0:T(8,128)S(1)} collective-permute-done((f32[128,2048]{1,0:T(8,128)S(1)}, f32[128,2048]{1,0:T(8,128)S(1)}, u32[]{:S(2)}, u32[]{:S(2)}) %collective-permute-start.2) | collective-permute-done | bytes 1048608 | tf_op jit(solution)/shard_map/ppermute | solution.py:240
  20.3 0.0 copy-done.3
  20.3 0.0 copy-done.4
  20.3 0.0 copy-done.1
  20.3 0.0 copy-start.2
  20.3 1.0 copy-done.2
  21.3 16.5 %shard_map.46.img_ref = f32[4,128,2048]{2,1,0:T(8,128)} custom-call(f32[8,256]{1,0:T(8,128)} %fusion.3.table_ref, f32[2,128,2048]{2,1,0:T(8,128)} %dnext_ref.1, f32[2,128,2048]{2,1,0:T(8,128)} %dnext_ref.1, f32[2,128,2048]{2,1,0:T(8,128)} %dnext_ref.1, f32[2,8,2048]{2,1,0:T(8,128)} %copy-done.4, f32[2,8,2048]{2,1,0:T(8,128)} %copy-done.3, ...), custom_call_target="tpu_custom_call" | custom-call | tf_op jit(solution)/shard_map/pallas_call | solution.py:107
  37.8 0.0 copy-start
  37.8 2.2 %copy-done = f32[4,128,2048]{2,1,0:T(8,128)S(1)} copy-done((f32[4,128,2048]{2,1,0:T(8,128)S(1)}, f32[4,128,2048]{2,1,0:T(8,128)}, u32[]{:S(2)}) %copy-start) | copy-done | bytes 4194328
  40.0 71.9 %shard_map.47 = f32[4,32,128]{2,1,0:T(8,128)S(1)} custom-call(f32[4,128,2048]{2,1,0:T(8,128)S(1)} %copy-done), custom_call_target="tpu_custom_call" | custom-call | tf_op jit(solution)/shard_map/pallas_call | solution.py:221
  111.9 0.6 copy.6
  (1 shorter events, 0.0 us)
Async XLA Ops:
  0.0 12.9 %copy-start.6 = (bf16[256]{0:T(256)(128)(2,1)S(1)}, bf16[256]{0:T(256)(128)(2,1)}, u32[]{:S(2)}) copy-start(bf16[256]{0:T(256)(128)(2,1)} %param.7) | copy-start | bytes 1540
  0.0 12.9 %copy-start.5 = (bf16[3,256]{1,0:T(4,128)(2,1)S(1)}, bf16[3,256]{1,0:T(4,128)(2,1)}, u32[]{:S(2)}) copy-start(bf16[3,256]{1,0:T(4,128)(2,1)} %param.6) | copy-start | bytes 4612
  1.7 15.0 %collective-permute-start.3 = (f32[128,2048]{1,0:T(8,128)S(1)}, f32[128,2048]{1,0:T(8,128)S(1)}, u32[]{:S(2)}, u32[]{:S(2)}) collective-permute-start(f32[128,2048]{1,0:T(8,128)S(1)} %get-tuple-element.5), channel_id=1, source_target_pairs={{4,0},{8,4},{12,8},{16,12},{20,16},{24,20},{28,24},{32,28},{36,32}... | collective-permute-start | bytes 3145736 | tf_op jit(solution)/shard_map/ppermute | solution.py:241
  3.6 16.7 %collective-permute-start.2 = (f32[128,2048]{1,0:T(8,128)S(1)}, f32[128,2048]{1,0:T(8,128)S(1)}, u32[]{:S(2)}, u32[]{:S(2)}) collective-permute-start(f32[128,2048]{1,0:T(8,128)S(1)} %get-tuple-element.6), channel_id=1, source_target_pairs={{0,4},{4,8},{8,12},{12,16},{16,20},{20,24},{24,28},{28,32},{32,36}... | collective-permute-start | bytes 3145736 | tf_op jit(solution)/shard_map/ppermute | solution.py:240
  7.1 8.0 %collective-permute-start.1 = (f32[2,8,2048]{2,1,0:T(8,128)S(1)}, f32[2,8,2048]{2,1,0:T(8,128)S(1)}, u32[]{:S(2)}, u32[]{:S(2)}) collective-permute-start(f32[2,8,2048]{2,1,0:T(8,128)S(1)} %get-tuple-element.7), channel_id=1, source_target_pairs={{1,0},{2,1},{3,2},{5,4},{6,5},{7,6},{9,8},{10,9},{11,10},{13,12},{... | collective-permute-start | bytes 393224 | tf_op jit(solution)/shard_map/ppermute | solution.py:243
  8.4 8.4 %collective-permute-start = (f32[2,8,2048]{2,1,0:T(8,128)S(1)}, f32[2,8,2048]{2,1,0:T(8,128)S(1)}, u32[]{:S(2)}, u32[]{:S(2)}) collective-permute-start(f32[2,8,2048]{2,1,0:T(8,128)S(1)} %get-tuple-element.8), channel_id=1, source_target_pairs={{0,1},{1,2},{2,3},{4,5},{5,6},{6,7},{8,9},{9,10},{10,11},{12,13},{... | collective-permute-start | bytes 393224 | tf_op jit(solution)/shard_map/ppermute | solution.py:242
  15.1 5.2 %copy-start.3 = (f32[2,8,2048]{2,1,0:T(8,128)}, f32[2,8,2048]{2,1,0:T(8,128)S(1)}, u32[]{:S(2)}) copy-start(f32[2,8,2048]{2,1,0:T(8,128)S(1)} %collective-permute-done.1.hbot_ref) | copy-start | bytes 393220
  16.7 3.6 %copy-start.4 = (f32[2,8,2048]{2,1,0:T(8,128)}, f32[2,8,2048]{2,1,0:T(8,128)S(1)}, u32[]{:S(2)}) copy-start(f32[2,8,2048]{2,1,0:T(8,128)S(1)} %collective-permute-done.htop_ref) | copy-start | bytes 393220
  16.8 3.6 %copy-start.1 = (f32[128,2048]{1,0:T(8,128)}, f32[128,2048]{1,0:T(8,128)S(1)}, u32[]{:S(2)}) copy-start(f32[128,2048]{1,0:T(8,128)S(1)} %collective-permute-done.3.xn_ref) | copy-start | bytes 3145732
  20.3 1.0 copy-start.2
  37.8 2.2 %copy-start = (f32[4,128,2048]{2,1,0:T(8,128)S(1)}, f32[4,128,2048]{2,1,0:T(8,128)}, u32[]{:S(2)}) copy-start(f32[4,128,2048]{2,1,0:T(8,128)} %shard_map.46.img_ref) | copy-start | bytes 12582916

commit v3 on v1

v3 whole, which is shorter than its diff:
```python
import functools

import jax
import jax.numpy as jnp
from jax import lax
from jax.experimental import pallas as pl
from jax.experimental.pallas import tpu as pltpu
from jax.sharding import PartitionSpec as P

ROW_BLOCK = 32
LANES = 128


def shift_pair(axis, count):
    return [(i, i + 1) for i in range(count - 1)], [(i + 1, i) for i in range(count - 1)]


def render_rows(depth_scale, tables, c, n_chunks, d_ref, htop_ref, hbot_ref, xp_ref, xn_ref, b_ref,
                img_ref):
    row_block = d_ref.shape[1] // n_chunks
    chunks = row_block // 8
    groups = d_ref.shape[2] // LANES
    base = c * row_block
    sub = lax.broadcasted_iota(jnp.int32, (8, LANES), 0)
    lane = lax.broadcasted_iota(jnp.int32, (8, LANES), 1)

    def look(idx):
        low = idx & (LANES - 1)
        high = idx >= LANES
        vals = []
        for lo_t, hi_t in tables:
            lo_v = jnp.take_along_axis(lo_t, low, axis=1, mode="promise_in_bounds")
            hi_v = jnp.take_along_axis(hi_t, low, axis=1, mode="promise_in_bounds")
            vals.append(jnp.where(high, hi_v, lo_v))
        return vals

    def group_body(g, carry):
        col = pl.ds(pl.multiple_of(g * LANES, LANES), LANES)
        col_l = pl.ds(pl.multiple_of(jnp.maximum(g - 1, 0) * LANES, LANES), LANES)
        col_r = pl.ds(pl.multiple_of(jnp.minimum(g + 1, groups - 1) * LANES, LANES), LANES)
        has_l = g > 0
        has_r = g < groups - 1
        centers = [[d_ref[p, pl.ds(base + k * 8, 8), col] for k in range(chunks)] for p in range(2)]
        for k in range(chunks):
            rows = pl.ds(base + k * 8, 8)
            samples = []
            for p in range(2):
                c_v = centers[p][k]
                if k > 0:
                    up_src = centers[p][k - 1]
                elif c == 0:
                    up_src = htop_ref[p, :, col]
                else:
                    up_src = d_ref[p, pl.ds(base - 8, 8), col]
                if k < chunks - 1:
                    dn_src = centers[p][k + 1]
                elif c == n_chunks - 1:
                    dn_src = hbot_ref[p, :, col]
                else:
                    dn_src = d_ref[p, pl.ds(base + row_block, 8), col]
                up = jnp.where(sub == 0, pltpu.roll(up_src, 1, 0), pltpu.roll(c_v, 1, 0))
                dn = jnp.where(sub == 7, pltpu.roll(dn_src, 7, 0), pltpu.roll(c_v, 7, 0))
                grad_y = (dn - up) * 0.5
                left_src = jnp.where(has_l, d_ref[p, rows, col_l], 0.0)
                right_src = jnp.where(has_r, d_ref[p, rows, col_r], 0.0)
                lf = jnp.where(lane == 0, pltpu.roll(left_src, 1, 1), pltpu.roll(c_v, 1, 1))
                rt = jnp.where(lane == LANES - 1, pltpu.roll(right_src, LANES - 1, 1),
                               pltpu.roll(c_v, LANES - 1, 1))
                grad_z = (rt - lf) * 0.5
                if p == 0:
                    grad_x = (centers[1][k] - xp_ref[rows, col]) * 0.5
                else:
                    grad_x = (xn_ref[rows, col] - centers[0][k]) * 0.5
                lit = jnp.abs(0.48 * grad_x + 0.6 * grad_y + 0.64 * grad_z)
                shade = 0.3 + 0.7 * lit / jnp.sqrt(
                    grad_x * grad_x + grad_y * grad_y + grad_z * grad_z + 1.0)
                entries = look(b_ref[p, rows, col])
                optical = entries[3] * depth_scale
                absorb = 1.0 - jnp.exp(-optical)
                emitted = [entries[ch] * shade * absorb for ch in range(3)]
                samples.append((optical, emitted))
            (o0, e0), (o1, e1) = samples
            t0 = jnp.exp(-o0)
            for ch in range(3):
                img_ref[ch, rows, col] = e0[ch] + t0 * e1[ch]
            img_ref[3, rows, col] = jnp.exp(-(o0 + o1))
        return carry

    lax.fori_loop(0, groups, group_body, 0)


def combine_lanes(dst_ref, src_ref, keep_off, rcv_ref, behind, row0, n_rows, half):
    lanes = min(half, LANES)
    groups = half // lanes

    def body(i, carry):
        r_sl = pl.ds(pl.multiple_of(row0 + i * 8, 8), 8)
        for j in range(groups):
            k_sl = pl.ds(pl.multiple_of(keep_off + j * lanes, lanes), lanes)
            d_sl = pl.ds(j * lanes, lanes)
            kept = [src_ref[ch, r_sl, k_sl] for ch in range(4)]
            rcv = [rcv_ref[ch, r_sl, d_sl] for ch in range(4)]
            front = [jnp.where(behind, q, k) for k, q in zip(kept, rcv)]
            back = [jnp.where(behind, k, q) for k, q in zip(kept, rcv)]
            for ch in range(3):
                dst_ref[ch, r_sl, d_sl] = front[ch] + front[3] * back[ch]
            dst_ref[3, r_sl, d_sl] = front[3] * back[3]
        return carry

    lax.fori_loop(0, n_rows // 8, body, 0)


def combine_rows(dst_ref, src_ref, keep_off, rcv_ref, behind, half, finish):
    def body(i, carry):
        r_k = pl.ds(pl.multiple_of(keep_off + i * 8, 8), 8)
        r_d = pl.ds(pl.multiple_of(i * 8, 8), 8)
        kept = [src_ref[ch, r_k, :] for ch in range(4)]
        rcv = [rcv_ref[ch, r_d, :] for ch in range(4)]
        front = [jnp.where(behind, q, k) for k, q in zip(kept, rcv)]
        back = [jnp.where(behind, k, q) for k, q in zip(kept, rcv)]
        for ch in range(3):
            dst_ref[ch, r_d, :] = front[ch] + front[3] * back[ch]
        trans = front[3] * back[3]
        dst_ref[3, r_d, :] = (1.0 - trans) if finish else trans
        return carry

    lax.fori_loop(0, half // 8, body, 0)


def fused_kernel(depth_scale, n_rounds, lane_rounds, n_chunks, table_ref, d_ref, htop_ref, hbot_ref,
                 xp_ref, xn_ref, b_ref, out_ref, img_ref, *scratch):
    recv = scratch[:n_rounds]
    acc = scratch[n_rounds:2 * n_rounds - 1]
    flip_ref = scratch[2 * n_rounds - 1]
    send_sems, recv_sems = scratch[2 * n_rounds:]
    me = lax.axis_index("depth")
    tile = lax.axis_index("tile")
    bits = [(me // (1 << r)) % 2 for r in range(n_rounds)]
    partners = [me + (1 - 2 * bits[r]) * (1 << r) for r in range(n_rounds)]
    rows = d_ref.shape[1]
    width = d_ref.shape[2]
    row_block = rows // n_chunks
    halves = [width >> (r + 1) for r in range(n_rounds)]
    srcs = [img_ref] + list(acc)

    barrier = pltpu.get_barrier_semaphore()
    for r in range(n_rounds):
        pl.semaphore_signal(barrier, inc=1, device_id=(partners[r], tile),
                            device_id_type=pl.DeviceIdType.MESH)
    pl.semaphore_wait(barrier, n_rounds)

    tables = [
        (jnp.broadcast_to(table_ref[ch:ch + 1, 0:LANES], (8, LANES)),
         jnp.broadcast_to(table_ref[ch:ch + 1, LANES:2 * LANES], (8, LANES)))
        for ch in range(4)
    ]
    copies = {}

    def start_lane(r, c):
        row_sl = pl.ds(c * row_block, row_block)
        send_off = pl.multiple_of((1 - bits[r]) * halves[r], LANES)
        copy = pltpu.make_async_remote_copy(
            src_ref=srcs[r].at[:, row_sl, pl.ds(send_off, halves[r])],
            dst_ref=recv[r].at[:, row_sl, :],
            send_sem=send_sems.at[r * n_chunks + c],
            recv_sem=recv_sems.at[r * n_chunks + c],
            device_id=(partners[r], tile),
            device_id_type=pl.DeviceIdType.MESH,
        )
        copy.start()
        copies[(r, c)] = copy

    def finish_lane(r, c):
        copies[(r, c)].wait()
        combine_lanes(acc[r], srcs[r], bits[r] * halves[r], recv[r], bits[r] == 1,
                      c * row_block, row_block, halves[r])
        if r + 1 < lane_rounds:
            start_lane(r + 1, c)

    for c in range(n_chunks):
        render_rows(depth_scale, tables, c, n_chunks, d_ref, htop_ref, hbot_ref, xp_ref, xn_ref,
                    b_ref, img_ref)
        start_lane(0, c)
        if c >= 1:
            finish_lane(0, c - 1)
    finish_lane(0, n_chunks - 1)
    for r in range(1, lane_rounds):
        for c in range(n_chunks):
            finish_lane(r, c)

    src = acc[lane_rounds - 1]
    for ch in range(4):
        flip_ref[ch] = src[ch].T
    src = flip_ref
    sem_base = lane_rounds * n_chunks
    for r in range(lane_rounds, n_rounds):
        half = halves[r]
        send_off = pl.multiple_of((1 - bits[r]) * half, 8)
        copy = pltpu.make_async_remote_copy(
            src_ref=src.at[:, pl.ds(send_off, half), :],
            dst_ref=recv[r],
            send_sem=send_sems.at[sem_base + r - lane_rounds],
            recv_sem=recv_sems.at[sem_base + r - lane_rounds],
            device_id=(partners[r], tile),
            device_id_type=pl.DeviceIdType.MESH,
        )
        copy.start()
        copy.wait()
        last = r == n_rounds - 1
        dst = out_ref if last else acc[r]
        combine_rows(dst, src, bits[r] * half, recv[r], bits[r] == 1, half, last)
        src = dst


def render_composite(density, bins, table, x_prev, x_next, h_top, h_bot, depth_scale, n_rounds):
    planes, rows, width = density.shape
    lane_rounds = 0
    while (width >> (lane_rounds + 1)) >= LANES and lane_rounds < n_rounds:
        lane_rounds += 1
    n_chunks = rows // ROW_BLOCK
    shapes = []
    for r in range(n_rounds):
        half = width >> (r + 1)
        shapes.append((4, rows, half) if r < lane_rounds else (4, half, rows))
    scratch = [pltpu.VMEM((4, rows, width), jnp.float32)]
    scratch += [pltpu.VMEM(s, jnp.float32) for s in shapes]
    scratch += [pltpu.VMEM(s, jnp.float32) for s in shapes[:-1]]
    scratch += [pltpu.VMEM((4, width >> lane_rounds, rows), jnp.float32)]
    n_sems = lane_rounds * n_chunks + n_rounds - lane_rounds
    scratch += [pltpu.SemaphoreType.DMA((n_sems,)), pltpu.SemaphoreType.DMA((n_sems,))]
    vmem = pl.BlockSpec(memory_space=pltpu.VMEM)
    out = pl.pallas_call(
        functools.partial(fused_kernel, depth_scale, n_rounds, lane_rounds, n_chunks),
        out_shape=jax.ShapeDtypeStruct(shapes[-1], jnp.float32),
        in_specs=[vmem] * 7,
        out_specs=vmem,
        scratch_shapes=scratch,
        compiler_params=pltpu.CompilerParams(
            collective_id=0, has_side_effects=True, vmem_limit_bytes=60 * 1024 * 1024),
    )(table, density, h_top, h_bot, x_prev, x_next, bins)
    return jnp.transpose(out, (0, 2, 1))


def per_device(density, bins, colors, extinction):
    depth_cells, row_cells, col_cells = density.shape
    slab_count = lax.axis_size("depth")
    tile_count = lax.axis_size("tile")
    depth_scale = 0.6 / (depth_cells * slab_count)
    fwd_d, bwd_d = shift_pair("depth", slab_count)
    fwd_t, bwd_t = shift_pair("tile", tile_count)
    x_prev = lax.ppermute(density[-1], "depth", fwd_d)
    x_next = lax.ppermute(density[0], "depth", bwd_d)
    h_top = lax.ppermute(density[:, row_cells - 8:], "tile", fwd_t)
    h_bot = lax.ppermute(density[:, :8], "tile", bwd_t)
    lookup = jnp.concatenate([colors, extinction[None, :]], 0).astype(jnp.float32)
    table = jnp.concatenate([lookup, jnp.zeros((4, lookup.shape[1]), jnp.float32)], 0)
    return render_composite(density, bins, table, x_prev, x_next, h_top, h_bot, depth_scale,
                            slab_count.bit_length() - 1)


def solution(mesh):
    return jax.shard_map(
        per_device,
        mesh=mesh,
        in_specs=(P("depth", "tile", None), P("depth", "tile", None), P(), P()),
        out_specs=P(None, "tile", "depth"),
        check_vma=False,
    )
```

time: 139 us -> 95.8 us (0.69); the launches traced: 137 us -> 95.6 us
  waiting for transfers between devices: 75.5 us -> 5.95 us
  Pallas kernels: 16.5 us -> 73.4 us
  starting transfers between devices: 27.4 us -> 10.3 us
  other arithmetic: 10.9 us -> 0.61 us
    ppermute x6 -> x0, waiting for transfers between devices: 70.2 us -> none  [partner(): lax.ppermute(value, axis, [(i, i ^ 1 << stride) for i in range(lax.axis_s...]
    pallas_call x1, Pallas kernels: 16.5 us -> 73.4 us  [render_composite(): pl.pallas_call(functools.partial(fused_kernel, depth_scale, n_rounds, lan...]
    ppermute x6 -> x0, starting transfers between devices: 17.2 us -> none  [partner(): lax.ppermute(value, axis, [(i, i ^ 1 << stride) for i in range(lax.axis_s...]
    select_n x12 -> x0, other arithmetic: 8.77 us -> none  [the longest x6 5.58 us: per_device(): front = jnp.where(behind, received, kept_part)]
  transfers between devices with their start and end apart: 10 -> 4, of which waited for: 9 -> 3; matrix products, arithmetic and copies ran while one was open for 2% -> 2% of each run, Pallas kernels for 0% -> 0%
where the time goes in v3:
time: 95.8 us; the launch traced here: 95.6 us
  Pallas kernels  73.4 us (77%)
  starting transfers between devices  10.3 us (11%)
  waiting for transfers between devices  5.95 us (6%)
  local copies, waits for them, and re-layouts  5.28 us (6%)
    pallas_call x1, Pallas kernels, render_composite(): pl.pallas_call(functools.partial(fused_kernel, depth_scale, n_rounds, lan...  73.4 us
    ppermute x1, waiting for transfers between devices, per_device(): h_bot = lax.ppermute(density[:, :8], 'tile', bwd_t)  4.12 us
    ppermute x1, starting transfers between devices, per_device(): x_next = lax.ppermute(density[0], 'depth', bwd_d)  3.64 us
    ppermute x1, starting transfers between devices, per_device(): h_top = lax.ppermute(density[:, row_cells - 8:], 'tile', fwd_t)  3.4 us
    unnamed x13, local copies, waits for them, and re-layouts  2.58 us
    ppermute x1, starting transfers between devices, per_device(): x_prev = lax.ppermute(density[-1], 'depth', fwd_d)  1.92 us
  transfers between devices with their start and end apart: 4, of which 3 were waited for; matrix products, arithmetic and copies ran while one was open for 2% of the time, Pallas kernels for 0%

profile of v3, /device:TPU:8, one launch (start us, length us, event | category | flops | bytes accessed | tf_op | source)
XLA Modules:
  0.0 95.6 jit_solution(9031027962484243618)
XLA Ops:
  0.0 0.0 copy-start.5
  0.0 0.0 copy-start.4
  0.0 1.7 %slice_bitcast_fusion = (f32[128,2048]{1,0:T(8,128)S(1)}, f32[128,2048]{1,0:T(8,128)S(1)}) fusion(f32[2,128,2048]{2,1,0:T(8,128)} %d_ref.1), kind=kLoop, calls=%fused_computation | loop fusion | bytes 4194304 | tf_op jit(solution)/shard_map/squeeze | solution.py:252
  1.7 1.9 %collective-permute-start.2 = (f32[128,2048]{1,0:T(8,128)S(1)}, f32[128,2048]{1,0:T(8,128)S(1)}, u32[]{:S(2)}, u32[]{:S(2)}) collective-permute-start(f32[128,2048]{1,0:T(8,128)S(1)} %get-tuple-element.6), channel_id=1, source_target_pairs={{0,4},{4,8},{8,12},{12,16},{16,20},{20,24},{24,28},{28,32},{32,36}... | collective-permute-start | bytes 3145736 | tf_op jit(solution)/shard_map/ppermute | solution.py:251
  3.6 3.6 %collective-permute-start.3 = (f32[128,2048]{1,0:T(8,128)S(1)}, f32[128,2048]{1,0:T(8,128)S(1)}, u32[]{:S(2)}, u32[]{:S(2)}) collective-permute-start(f32[128,2048]{1,0:T(8,128)S(1)} %get-tuple-element.5), channel_id=1, source_target_pairs={{4,0},{8,4},{12,8},{16,12},{20,16},{24,20},{28,24},{32,28},{36,32}... | collective-permute-start | bytes 3145736 | tf_op jit(solution)/shard_map/ppermute | solution.py:252
  7.3 1.0 %fusion.4 = (f32[2,8,2048]{2,1,0:T(8,128)S(1)}, f32[2,8,2048]{2,1,0:T(8,128)S(1)}) fusion(f32[2,128,2048]{2,1,0:T(8,128)} %d_ref.1), kind=kLoop, calls=%fused_computation.7 | loop fusion | bytes 524288 | tf_op jit(solution)/shard_map/slice | solution.py:254
  8.3 3.4 %collective-permute-start = (f32[2,8,2048]{2,1,0:T(8,128)S(1)}, f32[2,8,2048]{2,1,0:T(8,128)S(1)}, u32[]{:S(2)}, u32[]{:S(2)}) collective-permute-start(f32[2,8,2048]{2,1,0:T(8,128)S(1)} %get-tuple-element.8), channel_id=1, source_target_pairs={{0,1},{1,2},{2,3},{4,5},{5,6},{6,7},{8,9},{9,10},{10,11},{12,13},{... | collective-permute-start | bytes 393224 | tf_op jit(solution)/shard_map/ppermute | solution.py:253
  11.7 1.3 %collective-permute-start.1 = (f32[2,8,2048]{2,1,0:T(8,128)S(1)}, f32[2,8,2048]{2,1,0:T(8,128)S(1)}, u32[]{:S(2)}, u32[]{:S(2)}) collective-permute-start(f32[2,8,2048]{2,1,0:T(8,128)S(1)} %get-tuple-element.7), channel_id=1, source_target_pairs={{1,0},{2,1},{3,2},{5,4},{6,5},{7,6},{9,8},{10,9},{11,10},{13,12},{... | collective-permute-start | bytes 393224 | tf_op jit(solution)/shard_map/ppermute | solution.py:254
  13.0 0.0 copy-done.5
  13.0 0.0 copy-done.4
  13.0 0.6 fusion.3.table_ref
  13.6 0.9 collective-permute-done.htop_ref
  14.6 0.0 copy-start.2
  14.6 4.1 %collective-permute-done.1.hbot_ref = f32[2,8,2048]{2,1,0:T(8,128)S(1)} collective-permute-done((f32[2,8,2048]{2,1,0:T(8,128)S(1)}, f32[2,8,2048]{2,1,0:T(8,128)S(1)}, u32[]{:S(2)}, u32[]{:S(2)}) %collective-permute-start.1) | collective-permute-done | bytes 131104 | tf_op jit(solution)/shard_map/ppermute | solution.py:254
  18.7 0.0 copy-start.3
  18.7 0.0 collective-permute-done.2.xp_ref
  18.7 0.0 copy-start
  18.7 0.9 collective-permute-done.3.xn_ref
  19.6 0.0 copy-done.2
  19.6 0.0 copy-done.3
  19.6 0.1 copy-done
  19.7 0.0 copy-start.1
  19.7 1.0 %copy-done.1 = f32[128,2048]{1,0:T(8,128)} copy-done((f32[128,2048]{1,0:T(8,128)}, f32[128,2048]{1,0:T(8,128)S(1)}, u32[]{:S(2)}) %copy-start.1) | copy-done | bytes 1048600
  20.7 73.4 %shard_map.46 = f32[4,32,128]{2,1,0:T(8,128)} custom-call(f32[8,256]{1,0:T(8,128)} %fusion.3.table_ref, f32[2,128,2048]{2,1,0:T(8,128)} %d_ref.1, f32[2,8,2048]{2,1,0:T(8,128)} %copy-done.2, f32[2,8,2048]{2,1,0:T(8,128)} %copy-done.3, f32[128,2048]{1,0:T(8,128)} %copy-done, f32[128,2048]{1,0:T(8,128)} %copy-done.1, s32[2,128,2048]{2,1,0:T(8,128)} %b_ref.1), custom_call_target="tpu_custom_call" | custom-call | tf_op jit(solution)/shard_map/pallas_call | solution.py:232
  94.1 1.5 %copy.6 = f32[4,128,32]{1,2,0:T(8,128)} copy(f32[4,128,32]{1,2,0:T(8,128)} %bitcast.5) | data formatting | bytes 131072
  (1 shorter events, 0.0 us)
Async XLA Ops:
  0.0 13.0 %copy-start.5 = (bf16[256]{0:T(256)(128)(2,1)S(1)}, bf16[256]{0:T(256)(128)(2,1)}, u32[]{:S(2)}) copy-start(bf16[256]{0:T(256)(128)(2,1)} %param.7) | copy-start | bytes 1540
  0.0 13.0 %copy-start.4 = (bf16[3,256]{1,0:T(4,128)(2,1)S(1)}, bf16[3,256]{1,0:T(4,128)(2,1)}, u32[]{:S(2)}) copy-start(bf16[3,256]{1,0:T(4,128)(2,1)} %param.6) | copy-start | bytes 4612
  1.7 17.0 %collective-permute-start.2 = (f32[128,2048]{1,0:T(8,128)S(1)}, f32[128,2048]{1,0:T(8,128)S(1)}, u32[]{:S(2)}, u32[]{:S(2)}) collective-permute-start(f32[128,2048]{1,0:T(8,128)S(1)} %get-tuple-element.6), channel_id=1, source_target_pairs={{0,4},{4,8},{8,12},{12,16},{16,20},{20,24},{24,28},{28,32},{32,36}... | collective-permute-start | bytes 3145736 | tf_op jit(solution)/shard_map/ppermute | solution.py:251
  3.6 15.9 %collective-permute-start.3 = (f32[128,2048]{1,0:T(8,128)S(1)}, f32[128,2048]{1,0:T(8,128)S(1)}, u32[]{:S(2)}, u32[]{:S(2)}) collective-permute-start(f32[128,2048]{1,0:T(8,128)S(1)} %get-tuple-element.5), channel_id=1, source_target_pairs={{4,0},{8,4},{12,8},{16,12},{20,16},{24,20},{28,24},{32,28},{36,32}... | collective-permute-start | bytes 3145736 | tf_op jit(solution)/shard_map/ppermute | solution.py:252
  8.3 6.3 %collective-permute-start = (f32[2,8,2048]{2,1,0:T(8,128)S(1)}, f32[2,8,2048]{2,1,0:T(8,128)S(1)}, u32[]{:S(2)}, u32[]{:S(2)}) collective-permute-start(f32[2,8,2048]{2,1,0:T(8,128)S(1)} %get-tuple-element.8), channel_id=1, source_target_pairs={{0,1},{1,2},{2,3},{4,5},{5,6},{6,7},{8,9},{9,10},{10,11},{12,13},{... | collective-permute-start | bytes 393224 | tf_op jit(solution)/shard_map/ppermute | solution.py:253
  11.7 7.0 %collective-permute-start.1 = (f32[2,8,2048]{2,1,0:T(8,128)S(1)}, f32[2,8,2048]{2,1,0:T(8,128)S(1)}, u32[]{:S(2)}, u32[]{:S(2)}) collective-permute-start(f32[2,8,2048]{2,1,0:T(8,128)S(1)} %get-tuple-element.7), channel_id=1, source_target_pairs={{1,0},{2,1},{3,2},{5,4},{6,5},{7,6},{9,8},{10,9},{11,10},{13,12},{... | collective-permute-start | bytes 393224 | tf_op jit(solution)/shard_map/ppermute | solution.py:254
  14.6 5.0 %copy-start.2 = (f32[2,8,2048]{2,1,0:T(8,128)}, f32[2,8,2048]{2,1,0:T(8,128)S(1)}, u32[]{:S(2)}) copy-start(f32[2,8,2048]{2,1,0:T(8,128)S(1)} %collective-permute-done.htop_ref) | copy-start | bytes 393220
  18.7 0.9 copy-start.3
  18.7 1.0 %copy-start = (f32[128,2048]{1,0:T(8,128)}, f32[128,2048]{1,0:T(8,128)S(1)}, u32[]{:S(2)}) copy-start(f32[128,2048]{1,0:T(8,128)S(1)} %collective-permute-done.2.xp_ref) | copy-start | bytes 3145732
  19.7 1.0 %copy-start.1 = (f32[128,2048]{1,0:T(8,128)}, f32[128,2048]{1,0:T(8,128)S(1)}, u32[]{:S(2)}) copy-start(f32[128,2048]{1,0:T(8,128)S(1)} %collective-permute-done.3.xn_ref) | copy-start | bytes 3145732

commit v4 on v3

--- a/solution.py
+++ b/solution.py
@@ -11,19 +11,7 @@
 LANES = 128
 
 
-def shift_pair(axis, count):
-    return [(i, i + 1) for i in range(count - 1)], [(i + 1, i) for i in range(count - 1)]
-
-
-def render_rows(depth_scale, tables, c, n_chunks, d_ref, htop_ref, hbot_ref, xp_ref, xn_ref, b_ref,
-                img_ref):
-    row_block = d_ref.shape[1] // n_chunks
-    chunks = row_block // 8
-    groups = d_ref.shape[2] // LANES
-    base = c * row_block
-    sub = lax.broadcasted_iota(jnp.int32, (8, LANES), 0)
-    lane = lax.broadcasted_iota(jnp.int32, (8, LANES), 1)
-
+def make_look(tables):
     def look(idx):
         low = idx & (LANES - 1)
         high = idx >= LANES
@@ -34,6 +22,43 @@
             vals.append(jnp.where(high, hi_v, lo_v))
         return vals
 
+    return look
+
+
+def lookup_rows(depth_scale, look, b_ref, stash_ref, img_ref):
+    rows = b_ref.shape[1]
+    groups = b_ref.shape[2] // LANES
+
+    def body(i, carry):
+        g = i % groups
+        k = i // groups
+        col = pl.ds(pl.multiple_of(g * LANES, LANES), LANES)
+        r_sl = pl.ds(pl.multiple_of(k * 8, 8), 8)
+        e0 = look(b_ref[0, r_sl, col])
+        e1 = look(b_ref[1, r_sl, col])
+        o0 = e0[3] * depth_scale
+        o1 = e1[3] * depth_scale
+        a0 = 1.0 - jnp.exp(-o0)
+        a1 = 1.0 - jnp.exp(-o1)
+        t0 = jnp.exp(-o0)
+        for ch in range(3):
+            stash_ref[ch, r_sl, col] = e0[ch] * a0
+            stash_ref[3 + ch, r_sl, col] = t0 * (e1[ch] * a1)
+        img_ref[3, r_sl, col] = jnp.exp(-(o0 + o1))
+        return carry
+
+    lax.fori_loop(0, (rows // 8) * groups, body, 0)
+
+
+def shade_rows(c, n_chunks, d_ref, htop_ref, hbot_ref, xp_ref, xn_ref, has_top, has_bot,
+               has_prev, has_next, stash_ref, img_ref):
+    row_block = d_ref.shape[1] // n_chunks
+    chunks = row_block // 8
+    groups = d_ref.shape[2] // LANES
+    base = c * row_block
+    sub = lax.broadcasted_iota(jnp.int32, (8, LANES), 0)
+    lane = lax.broadcasted_iota(jnp.int32, (8, LANES), 1)
+
     def group_body(g, carry):
         col = pl.ds(pl.multiple_of(g * LANES, LANES), LANES)
         col_l = pl.ds(pl.multiple_of(jnp.maximum(g - 1, 0) * LANES, LANES), LANES)
@@ -43,19 +68,19 @@
         centers = [[d_ref[p, pl.ds(base + k * 8, 8), col] for k in range(chunks)] for p in range(2)]
         for k in range(chunks):
             rows = pl.ds(base + k * 8, 8)
-            samples = []
+            shades = []
             for p in range(2):
                 c_v = centers[p][k]
                 if k > 0:
                     up_src = centers[p][k - 1]
                 elif c == 0:
-                    up_src = htop_ref[p, :, col]
+                    up_src = jnp.where(has_top, htop_ref[p, :, col], 0.0)
                 else:
                     up_src = d_ref[p, pl.ds(base - 8, 8), col]
                 if k < chunks - 1:
                     dn_src = centers[p][k + 1]
                 elif c == n_chunks - 1:
-                    dn_src = hbot_ref[p, :, col]
+                    dn_src = jnp.where(has_bot, hbot_ref[p, :, col], 0.0)
                 else:
                     dn_src = d_ref[p, pl.ds(base + row_block, 8), col]
                 up = jnp.where(sub == 0, pltpu.roll(up_src, 1, 0), pltpu.roll(c_v, 1, 0))
@@ -68,22 +93,15 @@
                                pltpu.roll(c_v, LANES - 1, 1))
                 grad_z = (rt - lf) * 0.5
                 if p == 0:
-                    grad_x = (centers[1][k] - xp_ref[rows, col]) * 0.5
+                    grad_x = (centers[1][k] - jnp.where(has_prev, xp_ref[rows, col], 0.0)) * 0.5
                 else:
-                    grad_x = (xn_ref[rows, col] - centers[0][k]) * 0.5
+                    grad_x = (jnp.where(has_next, xn_ref[rows, col], 0.0) - centers[0][k]) * 0.5
                 lit = jnp.abs(0.48 * grad_x + 0.6 * grad_y + 0.64 * grad_z)
-                shade = 0.3 + 0.7 * lit / jnp.sqrt(
-                    grad_x * grad_x + grad_y * grad_y + grad_z * grad_z + 1.0)
-                entries = look(b_ref[p, rows, col])
-                optical = entries[3] * depth_scale
-                absorb = 1.0 - jnp.exp(-optical)
-                emitted = [entries[ch] * shade * absorb for ch in range(3)]
-                samples.append((optical, emitted))
-            (o0, e0), (o1, e1) = samples
-            t0 = jnp.exp(-o0)
+                shades.append(0.3 + 0.7 * lit / jnp.sqrt(
+                    grad_x * grad_x + grad_y * grad_y + grad_z * grad_z + 1.0))
             for ch in range(3):
-                img_ref[ch, rows, col] = e0[ch] + t0 * e1[ch]
-            img_ref[3, rows, col] = jnp.exp(-(o0 + o1))
+                img_ref[ch, rows, col] = (stash_ref[ch, rows, col] * shades[0]
+                                          + stash_ref[3 + ch, rows, col] * shades[1])
         return carry
 
     lax.fori_loop(0, groups, group_body, 0)
@@ -127,14 +145,16 @@
     lax.fori_loop(0, half // 8, body, 0)
 
 
-def fused_kernel(depth_scale, n_rounds, lane_rounds, n_chunks, table_ref, d_ref, htop_ref, hbot_ref,
-                 xp_ref, xn_ref, b_ref, out_ref, img_ref, *scratch):
+def fused_kernel(depth_scale, n_rounds, lane_rounds, n_chunks, table_ref, d_ref, b_ref, out_ref,
+                 img_ref, stash_ref, xp_ref, xn_ref, htop_ref, hbot_ref, halo_send, halo_recv, *scratch):
     recv = scratch[:n_rounds]
     acc = scratch[n_rounds:2 * n_rounds - 1]
     flip_ref = scratch[2 * n_rounds - 1]
     send_sems, recv_sems = scratch[2 * n_rounds:]
     me = lax.axis_index("depth")
     tile = lax.axis_index("tile")
+    n_slabs = lax.axis_size("depth")
+    n_tiles = lax.axis_size("tile")
     bits = [(me // (1 << r)) % 2 for r in range(n_rounds)]
     partners = [me + (1 - 2 * bits[r]) * (1 << r) for r in range(n_rounds)]
     rows = d_ref.shape[1]
@@ -142,18 +162,61 @@
     row_block = rows // n_chunks
     halves = [width >> (r + 1) for r in range(n_rounds)]
     srcs = [img_ref] + list(acc)
+    mesh_id = pl.DeviceIdType.MESH
+    has_prev = me > 0
+    has_next = me < n_slabs - 1
+    has_top = tile > 0
+    has_bot = tile < n_tiles - 1
+    odd = bits[0] == 1
+    extra_nb = jnp.where(odd, has_next, has_prev)
+    extra_id = jnp.where(odd, me + 1, me - 1)
 
     barrier = pltpu.get_barrier_semaphore()
     for r in range(n_rounds):
-        pl.semaphore_signal(barrier, inc=1, device_id=(partners[r], tile),
-                            device_id_type=pl.DeviceIdType.MESH)
-    pl.semaphore_wait(barrier, n_rounds)
+        pl.semaphore_signal(barrier, inc=1, device_id=(partners[r], tile), device_id_type=mesh_id)
+
+    @pl.when(extra_nb)
+    def _():
+        pl.semaphore_signal(barrier, inc=1, device_id=(extra_id, tile), device_id_type=mesh_id)
+
+    @pl.when(has_top)
+    def _():
+        pl.semaphore_signal(barrier, inc=1, device_id=(me, tile - 1), device_id_type=mesh_id)
+
+    @pl.when(has_bot)
+    def _():
+        pl.semaphore_signal(barrier, inc=1, device_id=(me, tile + 1), device_id_type=mesh_id)
+
+    n_greet = (n_rounds + extra_nb.astype(jnp.int32) + has_top.astype(jnp.int32)
+               + has_bot.astype(jnp.int32))
+    pl.semaphore_wait(barrier, n_greet)
+
+    halo_copies = [
+        (has_next, has_prev, pltpu.make_async_remote_copy(
+            src_ref=d_ref.at[1], dst_ref=xp_ref, send_sem=halo_send.at[0],
+            recv_sem=halo_recv.at[0], device_id=(me + 1, tile), device_id_type=mesh_id)),
+        (has_prev, has_next, pltpu.make_async_remote_copy(
+            src_ref=d_ref.at[0], dst_ref=xn_ref, send_sem=halo_send.at[1],
+            recv_sem=halo_recv.at[1], device_id=(me - 1, tile), device_id_type=mesh_id)),
+        (has_bot, has_top, pltpu.make_async_remote_copy(
+            src_ref=d_ref.at[:, pl.ds(rows - 8, 8), :], dst_ref=htop_ref, send_sem=halo_send.at[2],
+            recv_sem=halo_recv.at[2], device_id=(me, tile + 1), device_id_type=mesh_id)),
+        (has_top, has_bot, pltpu.make_async_remote_copy(
+            src_ref=d_ref.at[:, pl.ds(0, 8), :], dst_ref=hbot_ref, send_sem=halo_send.at[3],
+            recv_sem=halo_recv.at[3], device_id=(me, tile - 1), device_id_type=mesh_id)),
+    ]
+    for send_if, _, copy in halo_copies:
+        pl.when(send_if)(copy.start)
 
     tables = [
         (jnp.broadcast_to(table_ref[ch:ch + 1, 0:LANES], (8, LANES)),
          jnp.broadcast_to(table_ref[ch:ch + 1, LANES:2 * LANES], (8, LANES)))
         for ch in range(4)
     ]
+    lookup_rows(depth_scale, make_look(tables), b_ref, stash_ref, img_ref)
+    for send_if, recv_if, copy in halo_copies:
+        pl.when(send_if)(copy.wait_send)
+        pl.when(recv_if)(copy.wait_recv)
     copies = {}
 
     def start_lane(r, c):
@@ -178,8 +241,8 @@
             start_lane(r + 1, c)
 
     for c in range(n_chunks):
-        render_rows(depth_scale, tables, c, n_chunks, d_ref, htop_ref, hbot_ref, xp_ref, xn_ref,
-                    b_ref, img_ref)
+        shade_rows(c, n_chunks, d_ref, htop_ref, hbot_ref, xp_ref, xn_ref, has_top, has_bot,
+                   has_prev, has_next, stash_ref, img_ref)
         start_lane(0, c)
         if c >= 1:
             finish_lane(0, c - 1)
@@ -212,7 +275,7 @@
         src = dst
 
 
-def render_composite(density, bins, table, x_prev, x_next, h_top, h_bot, depth_scale, n_rounds):
+def render_composite(density, bins, table, depth_scale, n_rounds):
     planes, rows, width = density.shape
     lane_rounds = 0
     while (width >> (lane_rounds + 1)) >= LANES and lane_rounds < n_rounds:
@@ -222,7 +285,16 @@
     for r in range(n_rounds):
         half = width >> (r + 1)
         shapes.append((4, rows, half) if r < lane_rounds else (4, half, rows))
-    scratch = [pltpu.VMEM((4, rows, width), jnp.float32)]
+    scratch = [
+        pltpu.VMEM((4, rows, width), jnp.float32),
+        pltpu.VMEM((6, rows, width), jnp.float32),
+        pltpu.VMEM((rows, width), jnp.float32),
+        pltpu.VMEM((rows, width), jnp.float32),
+        pltpu.VMEM((planes, 8, width), jnp.float32),
+        pltpu.VMEM((planes, 8, width), jnp.float32),
+        pltpu.SemaphoreType.DMA((4,)),
+        pltpu.SemaphoreType.DMA((4,)),
+    ]
     scratch += [pltpu.VMEM(s, jnp.float32) for s in shapes]
     scratch += [pltpu.VMEM(s, jnp.float32) for s in shapes[:-1]]
     scratch += [pltpu.VMEM((4, width >> lane_rounds, rows), jnp.float32)]
@@ -232,30 +304,22 @@
     out = pl.pallas_call(
         functools.partial(fused_kernel, depth_scale, n_rounds, lane_rounds, n_chunks),
         out_shape=jax.ShapeDtypeStruct(shapes[-1], jnp.float32),
-        in_specs=[vmem] * 7,
+        in_specs=[vmem] * 3,
         out_specs=vmem,
         scratch_shapes=scratch,
         compiler_params=pltpu.CompilerParams(
-            collective_id=0, has_side_effects=True, vmem_limit_bytes=60 * 1024 * 1024),
-    )(table, density, h_top, h_bot, x_prev, x_next, bins)
+            collective_id=0, has_side_effects=True, vmem_limit_bytes=48 * 1024 * 1024),
+    )(table, density, bins)
     return jnp.transpose(out, (0, 2, 1))
 
 
 def per_device(density, bins, colors, extinction):
-    depth_cells, row_cells, col_cells = density.shape
+    depth_cells = density.shape[0]
     slab_count = lax.axis_size("depth")
-    tile_count = lax.axis_size("tile")
     depth_scale = 0.6 / (depth_cells * slab_count)
-    fwd_d, bwd_d = shift_pair("depth", slab_count)
-    fwd_t, bwd_t = shift_pair("tile", tile_count)
-    x_prev = lax.ppermute(density[-1], "depth", fwd_d)
-    x_next = lax.ppermute(density[0], "depth", bwd_d)
-    h_top = lax.ppermute(density[:, row_cells - 8:], "tile", fwd_t)
-    h_bot = lax.ppermute(density[:, :8], "tile", bwd_t)
     lookup = jnp.concatenate([colors, extinction[None, :]], 0).astype(jnp.float32)
     table = jnp.concatenate([lookup, jnp.zeros((4, lookup.shape[1]), jnp.float32)], 0)
-    return render_composite(density, bins, table, x_prev, x_next, h_top, h_bot, depth_scale,
-                            slab_count.bit_length() - 1)
+    return render_composite(density, bins, table, depth_scale, slab_count.bit_length() - 1)
 
 
 def solution(mesh):

time: 95.8 us -> 95.5 us (level)
  Pallas kernels: 73.4 us -> 89.2 us
  starting transfers between devices: 10.3 us -> 0 us
  waiting for transfers between devices: 5.95 us -> 0 us
    pallas_call x1, Pallas kernels: 73.4 us -> 89.2 us  [render_composite(): pl.pallas_call(functools.partial(fused_kernel, depth_scale, n_rounds, lan...]
    ppermute x4 -> x0, starting transfers between devices: 10.3 us -> none  [the longest x1 3.64 us: per_device(): x_next = lax.ppermute(density[0], 'depth', bwd_d)]
    ppermute x4 -> x0, waiting for transfers between devices: 5.95 us -> none  [the longest x1 4.12 us: per_device(): h_bot = lax.ppermute(density[:, :8], 'tile', bwd_t)]
    squeeze x1 -> x0, local copies, waits for them, and re-layouts: 1.7 us -> none  [per_device(): x_next = lax.ppermute(density[0], 'depth', bwd_d)]
    unnamed x13 -> x5, local copies, waits for them, and re-layouts: 2.58 us -> 3.81 us
    slice x1 -> x0, local copies, waits for them, and re-layouts: 0.99 us -> none  [per_device(): h_bot = lax.ppermute(density[:, :8], 'tile', bwd_t)]
  transfers between devices with their start and end apart: 4 -> 0, of which waited for: 3 -> 0; matrix products, arithmetic and copies ran while one was open for 2% -> 0% of each run, Pallas kernels for 0% -> 0%
where the time goes in v4:
time: 95.5 us; the launch traced here: 94.3 us
  Pallas kernels  89.2 us (93%)
  local copies, waits for them, and re-layouts  4.47 us (5%)
    pallas_call x1, Pallas kernels, render_composite(): pl.pallas_call(functools.partial(fused_kernel, depth_scale, n_rounds, lan...  89.2 us
    unnamed x5, local copies, waits for them, and re-layouts  3.81 us

profile of v4, /device:TPU:8, one launch (start us, length us, event | category | flops | bytes accessed | tf_op | source)
XLA Modules:
  0.0 94.3 jit_solution(10124371689785340864)
XLA Ops:
  0.0 0.7 broadcast_in_dim.4
  0.7 0.7 fusion.3.table_ref
  1.3 0.0 copy-start
  1.4 1.6 %copy-done = f32[2,128,2048]{2,1,0:T(8,128)S(1)} copy-done((f32[2,128,2048]{2,1,0:T(8,128)S(1)}, f32[2,128,2048]{2,1,0:T(8,128)}, u32[]{:S(2)}) %copy-start) | copy-done | bytes 2097176
  2.9 0.0 copy-start.1
  2.9 1.6 %copy-done.1 = s32[2,128,2048]{2,1,0:T(8,128)S(1)} copy-done((s32[2,128,2048]{2,1,0:T(8,128)S(1)}, s32[2,128,2048]{2,1,0:T(8,128)}, u32[]{:S(2)}) %copy-start.1) | copy-done | bytes 2097176
  4.5 89.2 %shard_map.46 = f32[4,32,128]{2,1,0:T(8,128)S(1)} custom-call(f32[8,256]{1,0:T(8,128)S(1)} %fusion.3.table_ref, f32[2,128,2048]{2,1,0:T(8,128)S(1)} %copy-done, s32[2,128,2048]{2,1,0:T(8,128)S(1)} %copy-done.1), custom_call_target="tpu_custom_call" | custom-call | tf_op jit(solution)/shard_map/pallas_call | solution.py:304
  93.7 0.6 copy.6
Async XLA Ops:
  1.3 1.6 %copy-start = (f32[2,128,2048]{2,1,0:T(8,128)S(1)}, f32[2,128,2048]{2,1,0:T(8,128)}, u32[]{:S(2)}) copy-start(f32[2,128,2048]{2,1,0:T(8,128)} %d_ref.1) | copy-start | bytes 6291460
  2.9 1.6 %copy-start.1 = (s32[2,128,2048]{2,1,0:T(8,128)S(1)}, s32[2,128,2048]{2,1,0:T(8,128)}, u32[]{:S(2)}) copy-start(s32[2,128,2048]{2,1,0:T(8,128)} %b_ref.1) | copy-start | bytes 6291460

commit v5 on v4

--- a/solution.py
+++ b/solution.py
@@ -7,7 +7,7 @@
 from jax.experimental.pallas import tpu as pltpu
 from jax.sharding import PartitionSpec as P
 
-ROW_BLOCK = 32
+ROW_BLOCK = 16
 LANES = 128
 
 

time: 95.5 us -> 93.5 us (0.979)
  Pallas kernels: 89.2 us -> 86.7 us
    pallas_call x1, Pallas kernels: 89.2 us -> 86.7 us  [render_composite(): pl.pallas_call(functools.partial(fused_kernel, depth_scale, n_rounds, lan...]
where the time goes in v5:
time: 93.5 us; the launch traced here: 91.9 us
  Pallas kernels  86.7 us (93%)
  local copies, waits for them, and re-layouts  4.47 us (5%)
    pallas_call x1, Pallas kernels, render_composite(): pl.pallas_call(functools.partial(fused_kernel, depth_scale, n_rounds, lan...  86.7 us
    unnamed x5, local copies, waits for them, and re-layouts  3.81 us

profile of v5, /device:TPU:8, one launch (start us, length us, event | category | flops | bytes accessed | tf_op | source)
XLA Modules:
  0.0 91.9 jit_solution(14780612830644950562)
XLA Ops:
  0.0 0.7 broadcast_in_dim.4
  0.7 0.7 fusion.3.table_ref
  1.3 0.0 copy-start
  1.4 1.6 %copy-done = f32[2,128,2048]{2,1,0:T(8,128)S(1)} copy-done((f32[2,128,2048]{2,1,0:T(8,128)S(1)}, f32[2,128,2048]{2,1,0:T(8,128)}, u32[]{:S(2)}) %copy-start) | copy-done | bytes 2097176
  2.9 0.0 copy-start.1
  2.9 1.6 %copy-done.1 = s32[2,128,2048]{2,1,0:T(8,128)S(1)} copy-done((s32[2,128,2048]{2,1,0:T(8,128)S(1)}, s32[2,128,2048]{2,1,0:T(8,128)}, u32[]{:S(2)}) %copy-start.1) | copy-done | bytes 2097176
  4.5 86.7 %shard_map.46 = f32[4,32,128]{2,1,0:T(8,128)S(1)} custom-call(f32[8,256]{1,0:T(8,128)S(1)} %fusion.3.table_ref, f32[2,128,2048]{2,1,0:T(8,128)S(1)} %copy-done, s32[2,128,2048]{2,1,0:T(8,128)S(1)} %copy-done.1), custom_call_target="tpu_custom_call" | custom-call | tf_op jit(solution)/shard_map/pallas_call | solution.py:304
  91.3 0.6 copy.6
Async XLA Ops:
  1.3 1.6 %copy-start = (f32[2,128,2048]{2,1,0:T(8,128)S(1)}, f32[2,128,2048]{2,1,0:T(8,128)}, u32[]{:S(2)}) copy-start(f32[2,128,2048]{2,1,0:T(8,128)} %d_ref.1) | copy-start | bytes 6291460
  2.9 1.6 %copy-start.1 = (s32[2,128,2048]{2,1,0:T(8,128)S(1)}, s32[2,128,2048]{2,1,0:T(8,128)}, u32[]{:S(2)}) copy-start(s32[2,128,2048]{2,1,0:T(8,128)} %b_ref.1) | copy-start | bytes 6291460

commit v6 on v5

--- a/solution.py
+++ b/solution.py
@@ -9,6 +9,8 @@
 
 ROW_BLOCK = 16
 LANES = 128
+LOOK_ROWS = 128
+SHADE_UNROLL = 2
 
 
 def make_look(tables):
@@ -29,25 +31,28 @@
     rows = b_ref.shape[1]
     groups = b_ref.shape[2] // LANES
 
+    per_step = min(LOOK_ROWS, rows) // 8
+
     def body(i, carry):
         g = i % groups
-        k = i // groups
+        k0 = (i // groups) * per_step
         col = pl.ds(pl.multiple_of(g * LANES, LANES), LANES)
-        r_sl = pl.ds(pl.multiple_of(k * 8, 8), 8)
-        e0 = look(b_ref[0, r_sl, col])
-        e1 = look(b_ref[1, r_sl, col])
-        o0 = e0[3] * depth_scale
-        o1 = e1[3] * depth_scale
-        a0 = 1.0 - jnp.exp(-o0)
-        a1 = 1.0 - jnp.exp(-o1)
-        t0 = jnp.exp(-o0)
-        for ch in range(3):
-            stash_ref[ch, r_sl, col] = e0[ch] * a0
-            stash_ref[3 + ch, r_sl, col] = t0 * (e1[ch] * a1)
-        img_ref[3, r_sl, col] = jnp.exp(-(o0 + o1))
+        for kk in range(per_step):
+            r_sl = pl.ds(pl.multiple_of((k0 + kk) * 8, 8), 8)
+            e0 = look(b_ref[0, r_sl, col])
+            e1 = look(b_ref[1, r_sl, col])
+            o0 = e0[3] * depth_scale
+            o1 = e1[3] * depth_scale
+            a0 = 1.0 - jnp.exp(-o0)
+            a1 = 1.0 - jnp.exp(-o1)
+            t0 = jnp.exp(-o0)
+            for ch in range(3):
+                stash_ref[ch, r_sl, col] = e0[ch] * a0
+                stash_ref[3 + ch, r_sl, col] = t0 * (e1[ch] * a1)
+            img_ref[3, r_sl, col] = jnp.exp(-(o0 + o1))
         return carry
 
-    lax.fori_loop(0, (rows // 8) * groups, body, 0)
+    lax.fori_loop(0, (rows // 8 // per_step) * groups, body, 0)
 
 
 def shade_rows(c, n_chunks, d_ref, htop_ref, hbot_ref, xp_ref, xn_ref, has_top, has_bot,
@@ -104,7 +109,7 @@
                                           + stash_ref[3 + ch, rows, col] * shades[1])
         return carry
 
-    lax.fori_loop(0, groups, group_body, 0)
+    lax.fori_loop(0, groups, group_body, 0, unroll=SHADE_UNROLL)
 
 
 def combine_lanes(dst_ref, src_ref, keep_off, rcv_ref, behind, row0, n_rows, half):

time: 93.5 us -> 82.6 us (0.88)
  Pallas kernels: 86.7 us -> 76.2 us
    pallas_call x1, Pallas kernels: 86.7 us -> 76.2 us  [render_composite(): pl.pallas_call(functools.partial(fused_kernel, depth_scale, n_rounds, lan...]
where the time goes in v6:
time: 82.6 us; the launch traced here: 81.3 us
  Pallas kernels  76.2 us (92%)
  local copies, waits for them, and re-layouts  4.47 us (5%)
    pallas_call x1, Pallas kernels, render_composite(): pl.pallas_call(functools.partial(fused_kernel, depth_scale, n_rounds, lan...  76.2 us
    unnamed x5, local copies, waits for them, and re-layouts  3.81 us

profile of v6, /device:TPU:8, one launch (start us, length us, event | category | flops | bytes accessed | tf_op | source)
XLA Modules:
  0.0 81.3 jit_solution(7450184968831836329)
XLA Ops:
  0.0 0.7 broadcast_in_dim.4
  0.7 0.7 fusion.3.table_ref
  1.3 0.0 copy-start
  1.4 1.6 %copy-done = f32[2,128,2048]{2,1,0:T(8,128)S(1)} copy-done((f32[2,128,2048]{2,1,0:T(8,128)S(1)}, f32[2,128,2048]{2,1,0:T(8,128)}, u32[]{:S(2)}) %copy-start) | copy-done | bytes 2097176
  2.9 0.0 copy-start.1
  2.9 1.6 %copy-done.1 = s32[2,128,2048]{2,1,0:T(8,128)S(1)} copy-done((s32[2,128,2048]{2,1,0:T(8,128)S(1)}, s32[2,128,2048]{2,1,0:T(8,128)}, u32[]{:S(2)}) %copy-start.1) | copy-done | bytes 2097176
  4.5 76.2 %shard_map.46 = f32[4,32,128]{2,1,0:T(8,128)S(1)} custom-call(f32[8,256]{1,0:T(8,128)S(1)} %fusion.3.table_ref, f32[2,128,2048]{2,1,0:T(8,128)S(1)} %copy-done, s32[2,128,2048]{2,1,0:T(8,128)S(1)} %copy-done.1), custom_call_target="tpu_custom_call" | custom-call | tf_op jit(solution)/shard_map/pallas_call | solution.py:309
  80.7 0.6 copy.6
Async XLA Ops:
  1.3 1.6 %copy-start = (f32[2,128,2048]{2,1,0:T(8,128)S(1)}, f32[2,128,2048]{2,1,0:T(8,128)}, u32[]{:S(2)}) copy-start(f32[2,128,2048]{2,1,0:T(8,128)} %d_ref.1) | copy-start | bytes 6291460
  2.9 1.6 %copy-start.1 = (s32[2,128,2048]{2,1,0:T(8,128)S(1)}, s32[2,128,2048]{2,1,0:T(8,128)}, u32[]{:S(2)}) copy-start(s32[2,128,2048]{2,1,0:T(8,128)} %b_ref.1) | copy-start | bytes 6291460

commit v7 on v6

--- a/solution.py
+++ b/solution.py
@@ -9,7 +9,7 @@
 
 ROW_BLOCK = 16
 LANES = 128
-LOOK_ROWS = 128
+LOOK_UNROLL = 4
 SHADE_UNROLL = 2
 
 
@@ -27,18 +27,14 @@
     return look
 
 
-def lookup_rows(depth_scale, look, b_ref, stash_ref, img_ref):
-    rows = b_ref.shape[1]
+def lookup_rows(depth_scale, look, b_ref, stash_ref, img_ref, row0, n_rows):
     groups = b_ref.shape[2] // LANES
-
-    per_step = min(LOOK_ROWS, rows) // 8
-
-    def body(i, carry):
-        g = i % groups
-        k0 = (i // groups) * per_step
+    per_step = n_rows // 8
+
+    def body(g, carry):
         col = pl.ds(pl.multiple_of(g * LANES, LANES), LANES)
         for kk in range(per_step):
-            r_sl = pl.ds(pl.multiple_of((k0 + kk) * 8, 8), 8)
+            r_sl = pl.ds(row0 + kk * 8, 8)
             e0 = look(b_ref[0, r_sl, col])
             e1 = look(b_ref[1, r_sl, col])
             o0 = e0[3] * depth_scale
@@ -52,7 +48,7 @@
             img_ref[3, r_sl, col] = jnp.exp(-(o0 + o1))
         return carry
 
-    lax.fori_loop(0, (rows // 8 // per_step) * groups, body, 0)
+    lax.fori_loop(0, groups, body, 0, unroll=LOOK_UNROLL)
 
 
 def shade_rows(c, n_chunks, d_ref, htop_ref, hbot_ref, xp_ref, xn_ref, has_top, has_bot,
@@ -196,21 +192,26 @@
                + has_bot.astype(jnp.int32))
     pl.semaphore_wait(barrier, n_greet)
 
-    halo_copies = [
-        (has_next, has_prev, pltpu.make_async_remote_copy(
-            src_ref=d_ref.at[1], dst_ref=xp_ref, send_sem=halo_send.at[0],
-            recv_sem=halo_recv.at[0], device_id=(me + 1, tile), device_id_type=mesh_id)),
-        (has_prev, has_next, pltpu.make_async_remote_copy(
-            src_ref=d_ref.at[0], dst_ref=xn_ref, send_sem=halo_send.at[1],
-            recv_sem=halo_recv.at[1], device_id=(me - 1, tile), device_id_type=mesh_id)),
-        (has_bot, has_top, pltpu.make_async_remote_copy(
-            src_ref=d_ref.at[:, pl.ds(rows - 8, 8), :], dst_ref=htop_ref, send_sem=halo_send.at[2],
-            recv_sem=halo_recv.at[2], device_id=(me, tile + 1), device_id_type=mesh_id)),
-        (has_top, has_bot, pltpu.make_async_remote_copy(
-            src_ref=d_ref.at[:, pl.ds(0, 8), :], dst_ref=hbot_ref, send_sem=halo_send.at[3],
-            recv_sem=halo_recv.at[3], device_id=(me, tile - 1), device_id_type=mesh_id)),
+    def halo(send_if, recv_if, src_ref, dst_ref, idx, dev):
+        return (send_if, recv_if, pltpu.make_async_remote_copy(
+            src_ref=src_ref, dst_ref=dst_ref, send_sem=halo_send.at[idx],
+            recv_sem=halo_recv.at[idx], device_id=dev, device_id_type=mesh_id))
+
+    edge_copies = [
+        halo(has_bot, has_top, d_ref.at[:, pl.ds(rows - 8, 8), :], htop_ref, 0, (me, tile + 1)),
+        halo(has_top, has_bot, d_ref.at[:, pl.ds(0, 8), :], hbot_ref, 1, (me, tile - 1)),
     ]
-    for send_if, _, copy in halo_copies:
+    plane_copies = []
+    for c in range(n_chunks):
+        row_sl = pl.ds(c * row_block, row_block)
+        plane_copies.append((
+            halo(has_next, has_prev, d_ref.at[1, row_sl, :], xp_ref.at[row_sl, :], 2 + 2 * c,
+                 (me + 1, tile)),
+            halo(has_prev, has_next, d_ref.at[0, row_sl, :], xn_ref.at[row_sl, :], 3 + 2 * c,
+                 (me - 1, tile)),
+        ))
+    all_halos = edge_copies + [h for pair in plane_copies for h in pair]
+    for send_if, _, copy in all_halos:
         pl.when(send_if)(copy.start)
 
     tables = [
@@ -218,10 +219,7 @@
          jnp.broadcast_to(table_ref[ch:ch + 1, LANES:2 * LANES], (8, LANES)))
         for ch in range(4)
     ]
-    lookup_rows(depth_scale, make_look(tables), b_ref, stash_ref, img_ref)
-    for send_if, recv_if, copy in halo_copies:
-        pl.when(send_if)(copy.wait_send)
-        pl.when(recv_if)(copy.wait_recv)
+    look = make_look(tables)
     copies = {}
 
     def start_lane(r, c):
@@ -246,6 +244,14 @@
             start_lane(r + 1, c)
 
     for c in range(n_chunks):
+        lookup_rows(depth_scale, look, b_ref, stash_ref, img_ref, c * row_block, row_block)
+        waits = list(plane_copies[c])
+        if c == 0:
+            waits.append(edge_copies[0])
+        if c == n_chunks - 1:
+            waits.append(edge_copies[1])
+        for _, recv_if, copy in waits:
+            pl.when(recv_if)(copy.wait_recv)
         shade_rows(c, n_chunks, d_ref, htop_ref, hbot_ref, xp_ref, xn_ref, has_top, has_bot,
                    has_prev, has_next, stash_ref, img_ref)
         start_lane(0, c)
@@ -255,6 +261,8 @@
     for r in range(1, lane_rounds):
         for c in range(n_chunks):
             finish_lane(r, c)
+    for send_if, _, copy in all_halos:
+        pl.when(send_if)(copy.wait_send)
 
     src = acc[lane_rounds - 1]
     for ch in range(4):
@@ -297,8 +305,8 @@
         pltpu.VMEM((rows, width), jnp.float32),
         pltpu.VMEM((planes, 8, width), jnp.float32),
         pltpu.VMEM((planes, 8, width), jnp.float32),
-        pltpu.SemaphoreType.DMA((4,)),
-        pltpu.SemaphoreType.DMA((4,)),
+        pltpu.SemaphoreType.DMA((2 + 2 * n_chunks,)),
+        pltpu.SemaphoreType.DMA((2 + 2 * n_chunks,)),
     ]
     scratch += [pltpu.VMEM(s, jnp.float32) for s in shapes]
     scratch += [pltpu.VMEM(s, jnp.float32) for s in shapes[:-1]]

time: 82.6 us -> 78.4 us (0.949)
  Pallas kernels: 76.2 us -> 72.2 us
    pallas_call x1, Pallas kernels: 76.2 us -> 72.2 us  [render_composite(): pl.pallas_call(functools.partial(fused_kernel, depth_scale, n_rounds, lan...]
where the time goes in v7:
time: 78.4 us; the launch traced here: 77.3 us
  Pallas kernels  72.2 us (92%)
  local copies, waits for them, and re-layouts  4.47 us (6%)
    pallas_call x1, Pallas kernels, render_composite(): pl.pallas_call(functools.partial(fused_kernel, depth_scale, n_rounds, lan...  72.2 us
    unnamed x5, local copies, waits for them, and re-layouts  3.81 us

profile of v7, /device:TPU:8, one launch (start us, length us, event | category | flops | bytes accessed | tf_op | source)
XLA Modules:
  0.0 77.3 jit_solution(14519995838515792421)
XLA Ops:
  0.0 0.7 broadcast_in_dim.4
  0.7 0.7 fusion.3.table_ref
  1.3 0.0 copy-start
  1.4 1.6 %copy-done = f32[2,128,2048]{2,1,0:T(8,128)S(1)} copy-done((f32[2,128,2048]{2,1,0:T(8,128)S(1)}, f32[2,128,2048]{2,1,0:T(8,128)}, u32[]{:S(2)}) %copy-start) | copy-done | bytes 2097176
  2.9 0.0 copy-start.1
  2.9 1.6 %copy-done.1 = s32[2,128,2048]{2,1,0:T(8,128)S(1)} copy-done((s32[2,128,2048]{2,1,0:T(8,128)S(1)}, s32[2,128,2048]{2,1,0:T(8,128)}, u32[]{:S(2)}) %copy-start.1) | copy-done | bytes 2097176
  4.5 72.2 %shard_map.46 = f32[4,32,128]{2,1,0:T(8,128)S(1)} custom-call(f32[8,256]{1,0:T(8,128)S(1)} %fusion.3.table_ref, f32[2,128,2048]{2,1,0:T(8,128)S(1)} %copy-done, s32[2,128,2048]{2,1,0:T(8,128)S(1)} %copy-done.1), custom_call_target="tpu_custom_call" | custom-call | tf_op jit(solution)/shard_map/pallas_call | solution.py:317
  76.7 0.6 copy.6
Async XLA Ops:
  1.3 1.6 %copy-start = (f32[2,128,2048]{2,1,0:T(8,128)S(1)}, f32[2,128,2048]{2,1,0:T(8,128)}, u32[]{:S(2)}) copy-start(f32[2,128,2048]{2,1,0:T(8,128)} %d_ref.1) | copy-start | bytes 6291460
  2.9 1.6 %copy-start.1 = (s32[2,128,2048]{2,1,0:T(8,128)S(1)}, s32[2,128,2048]{2,1,0:T(8,128)}, u32[]{:S(2)}) copy-start(s32[2,128,2048]{2,1,0:T(8,128)} %b_ref.1) | copy-start | bytes 6291460

commit v8 on v7

--- a/solution.py
+++ b/solution.py
@@ -151,7 +151,7 @@
     recv = scratch[:n_rounds]
     acc = scratch[n_rounds:2 * n_rounds - 1]
     flip_ref = scratch[2 * n_rounds - 1]
-    send_sems, recv_sems = scratch[2 * n_rounds:]
+    send_sems, recv_sems, parts_ref, tail_send, tail_recv = scratch[2 * n_rounds:]
     me = lax.axis_index("depth")
     tile = lax.axis_index("tile")
     n_slabs = lax.axis_size("depth")
@@ -188,7 +188,14 @@
     def _():
         pl.semaphore_signal(barrier, inc=1, device_id=(me, tile + 1), device_id_type=mesh_id)
 
-    n_greet = (n_rounds + extra_nb.astype(jnp.int32) + has_top.astype(jnp.int32)
+    direct = n_rounds - lane_rounds == 2
+    group_step = 1 << lane_rounds
+    member = (me // group_step) % 4
+    group_base = me - member * group_step
+    if direct:
+        pl.semaphore_signal(barrier, inc=1, device_id=(group_base + (3 - member) * group_step, tile),
+                            device_id_type=mesh_id)
+    n_greet = (n_rounds + int(direct) + extra_nb.astype(jnp.int32) + has_top.astype(jnp.int32)
                + has_bot.astype(jnp.int32))
     pl.semaphore_wait(barrier, n_greet)
 
@@ -268,6 +275,47 @@
     for ch in range(4):
         flip_ref[ch] = src[ch].T
     src = flip_ref
+    if direct:
+        quarter = halves[-1]
+
+        def owned(j):
+            return (2 * (j % 2) + j // 2) * quarter
+
+        sends = []
+        for k in range(1, 4):
+            dst_j = (member + k) % 4
+            copy = pltpu.make_async_remote_copy(
+                src_ref=flip_ref.at[:, pl.ds(pl.multiple_of(owned(dst_j), 8), quarter), :],
+                dst_ref=parts_ref.at[member],
+                send_sem=tail_send.at[k - 1],
+                recv_sem=tail_recv.at[member],
+                device_id=(group_base + dst_j * group_step, tile),
+                device_id_type=mesh_id,
+            )
+            copy.start()
+            sends.append(copy)
+        parts_ref[member] = flip_ref[:, pl.ds(pl.multiple_of(owned(member), 8), quarter), :]
+        for k in range(1, 4):
+            src_j = (member + 4 - k) % 4
+            pltpu.make_async_remote_copy(
+                src_ref=flip_ref.at[:, pl.ds(0, quarter), :],
+                dst_ref=parts_ref.at[src_j],
+                send_sem=tail_send.at[k - 1],
+                recv_sem=tail_recv.at[src_j],
+                device_id=(group_base + src_j * group_step, tile),
+                device_id_type=mesh_id,
+            ).wait_recv()
+        for copy in sends:
+            copy.wait_send()
+        front = [parts_ref[0, ch] for ch in range(4)]
+        for j in range(1, 4):
+            back = [parts_ref[j, ch] for ch in range(4)]
+            front = [front[ch] + front[3] * back[ch] for ch in range(3)] + [front[3] * back[3]]
+        for ch in range(3):
+            out_ref[ch] = front[ch]
+        out_ref[3] = 1.0 - front[3]
+        return
+
     sem_base = lane_rounds * n_chunks
     for r in range(lane_rounds, n_rounds):
         half = halves[r]
@@ -313,6 +361,8 @@
     scratch += [pltpu.VMEM((4, width >> lane_rounds, rows), jnp.float32)]
     n_sems = lane_rounds * n_chunks + n_rounds - lane_rounds
     scratch += [pltpu.SemaphoreType.DMA((n_sems,)), pltpu.SemaphoreType.DMA((n_sems,))]
+    scratch += [pltpu.VMEM((4,) + shapes[-1], jnp.float32), pltpu.SemaphoreType.DMA((3,)),
+                pltpu.SemaphoreType.DMA((4,))]
     vmem = pl.BlockSpec(memory_space=pltpu.VMEM)
     out = pl.pallas_call(
         functools.partial(fused_kernel, depth_scale, n_rounds, lane_rounds, n_chunks),

time: 78.4 us -> 72.3 us (0.922)
  Pallas kernels: 72.2 us -> 66.7 us
    pallas_call x1, Pallas kernels: 72.2 us -> 66.7 us  [render_composite(): pl.pallas_call(functools.partial(fused_kernel, depth_scale, n_rounds, lan...]
where the time goes in v8:
time: 72.3 us; the launch traced here: 71.9 us
  Pallas kernels  66.7 us (92%)
  local copies, waits for them, and re-layouts  4.47 us (6%)
    pallas_call x1, Pallas kernels, render_composite(): pl.pallas_call(functools.partial(fused_kernel, depth_scale, n_rounds, lan...  66.7 us
    unnamed x5, local copies, waits for them, and re-layouts  3.81 us

profile of v8, /device:TPU:8, one launch (start us, length us, event | category | flops | bytes accessed | tf_op | source)
XLA Modules:
  0.0 71.9 jit_solution(13194302868339498139)
XLA Ops:
  0.0 0.7 broadcast_in_dim.4
  0.7 0.7 fusion.3.table_ref
  1.3 0.0 copy-start
  1.4 1.6 %copy-done = f32[2,128,2048]{2,1,0:T(8,128)S(1)} copy-done((f32[2,128,2048]{2,1,0:T(8,128)S(1)}, f32[2,128,2048]{2,1,0:T(8,128)}, u32[]{:S(2)}) %copy-start) | copy-done | bytes 2097176
  2.9 0.0 copy-start.1
  2.9 1.6 %copy-done.1 = s32[2,128,2048]{2,1,0:T(8,128)S(1)} copy-done((s32[2,128,2048]{2,1,0:T(8,128)S(1)}, s32[2,128,2048]{2,1,0:T(8,128)}, u32[]{:S(2)}) %copy-start.1) | copy-done | bytes 2097176
  4.5 66.7 %shard_map.46 = f32[4,32,128]{2,1,0:T(8,128)S(1)} custom-call(f32[8,256]{1,0:T(8,128)S(1)} %fusion.3.table_ref, f32[2,128,2048]{2,1,0:T(8,128)S(1)} %copy-done, s32[2,128,2048]{2,1,0:T(8,128)S(1)} %copy-done.1), custom_call_target="tpu_custom_call" | custom-call | tf_op jit(solution)/shard_map/pallas_call | solution.py:367
  71.3 0.6 copy.6
Async XLA Ops:
  1.3 1.6 %copy-start = (f32[2,128,2048]{2,1,0:T(8,128)S(1)}, f32[2,128,2048]{2,1,0:T(8,128)}, u32[]{:S(2)}) copy-start(f32[2,128,2048]{2,1,0:T(8,128)} %d_ref.1) | copy-start | bytes 6291460
  2.9 1.6 %copy-start.1 = (s32[2,128,2048]{2,1,0:T(8,128)S(1)}, s32[2,128,2048]{2,1,0:T(8,128)}, u32[]{:S(2)}) copy-start(s32[2,128,2048]{2,1,0:T(8,128)} %b_ref.1) | copy-start | bytes 6291460

commit v9 on v8

--- a/solution.py
+++ b/solution.py
@@ -151,7 +151,7 @@
     recv = scratch[:n_rounds]
     acc = scratch[n_rounds:2 * n_rounds - 1]
     flip_ref = scratch[2 * n_rounds - 1]
-    send_sems, recv_sems, parts_ref, tail_send, tail_recv = scratch[2 * n_rounds:]
+    send_sems, recv_sems, parts_ref, tail_send, tail_recv, y_parts, y_send, y_recv = scratch[2 * n_rounds:]
     me = lax.axis_index("depth")
     tile = lax.axis_index("tile")
     n_slabs = lax.axis_size("depth")
@@ -195,7 +195,13 @@
     if direct:
         pl.semaphore_signal(barrier, inc=1, device_id=(group_base + (3 - member) * group_step, tile),
                             device_id_type=mesh_id)
-    n_greet = (n_rounds + int(direct) + extra_nb.astype(jnp.int32) + has_top.astype(jnp.int32)
+    y_direct = lane_rounds >= 3
+    y_member = (me // 2) % 4
+    y_base = me - y_member * 2
+    if y_direct:
+        pl.semaphore_signal(barrier, inc=1, device_id=(y_base + (3 - y_member) * 2, tile),
+                            device_id_type=mesh_id)
+    n_greet = (n_rounds + int(direct) + int(y_direct) + extra_nb.astype(jnp.int32) + has_top.astype(jnp.int32)
                + has_bot.astype(jnp.int32))
     pl.semaphore_wait(barrier, n_greet)
 
@@ -243,11 +249,71 @@
         copy.start()
         copies[(r, c)] = copy
 
+    y_quarter = halves[2]
+
+    def y_owned(j):
+        return (j % 2) * halves[1] + (j // 2) * y_quarter
+
+    y_sends = []
+
+    def start_y(c):
+        row_sl = pl.ds(c * row_block, row_block)
+        for k in range(1, 4):
+            dst_j = (y_member + k) % 4
+            copy = pltpu.make_async_remote_copy(
+                src_ref=acc[0].at[:, row_sl, pl.ds(pl.multiple_of(y_owned(dst_j), LANES), y_quarter)],
+                dst_ref=y_parts.at[y_member, :, row_sl, :],
+                send_sem=y_send.at[(k - 1) * n_chunks + c],
+                recv_sem=y_recv.at[y_member * n_chunks + c],
+                device_id=(y_base + dst_j * 2, tile),
+                device_id_type=mesh_id,
+            )
+            copy.start()
+            y_sends.append(copy)
+
+    def finish_y(c):
+        row_sl = pl.ds(c * row_block, row_block)
+        for k in range(1, 4):
+            src_j = (y_member + 4 - k) % 4
+            pltpu.make_async_remote_copy(
+                src_ref=acc[0].at[:, row_sl, pl.ds(0, y_quarter)],
+                dst_ref=y_parts.at[src_j, :, row_sl, :],
+                send_sem=y_send.at[(k - 1) * n_chunks + c],
+                recv_sem=y_recv.at[src_j * n_chunks + c],
+                device_id=(y_base + src_j * 2, tile),
+                device_id_type=mesh_id,
+            ).wait_recv()
+        own = pl.multiple_of(y_owned(y_member), LANES)
+
+        def body(i, carry):
+            r_sl = pl.ds(pl.multiple_of(c * row_block + i * 8, 8), 8)
+            for g in range(y_quarter // LANES):
+                col = pl.ds(g * LANES, LANES)
+                own_col = pl.ds(pl.multiple_of(own + g * LANES, LANES), LANES)
+                parts = []
+                for j in range(4):
+                    mine = [acc[0][ch, r_sl, own_col] for ch in range(4)]
+                    got = [y_parts[j, ch, r_sl, col] for ch in range(4)]
+                    parts.append([jnp.where(y_member == j, m, q) for m, q in zip(mine, got)])
+                front = parts[0]
+                for back in parts[1:]:
+                    front = ([front[ch] + front[3] * back[ch] for ch in range(3)]
+                             + [front[3] * back[3]])
+                for ch in range(4):
+                    acc[2][ch, r_sl, col] = front[ch]
+            return carry
+
+        lax.fori_loop(0, row_block // 8, body, 0)
+        if lane_rounds > 3:
+            start_lane(3, c)
+
     def finish_lane(r, c):
         copies[(r, c)].wait()
         combine_lanes(acc[r], srcs[r], bits[r] * halves[r], recv[r], bits[r] == 1,
                       c * row_block, row_block, halves[r])
-        if r + 1 < lane_rounds:
+        if y_direct and r == 0:
+            start_y(c)
+        elif r + 1 < lane_rounds:
             start_lane(r + 1, c)
 
     for c in range(n_chunks):
@@ -267,7 +333,14 @@
     finish_lane(0, n_chunks - 1)
     for r in range(1, lane_rounds):
         for c in range(n_chunks):
-            finish_lane(r, c)
+            if y_direct and r == 1:
+                finish_y(c)
+            elif y_direct and r == 2:
+                continue
+            else:
+                finish_lane(r, c)
+    for copy in y_sends:
+        copy.wait_send()
     for send_if, _, copy in all_halos:
         pl.when(send_if)(copy.wait_send)
 
@@ -363,6 +436,9 @@
     scratch += [pltpu.SemaphoreType.DMA((n_sems,)), pltpu.SemaphoreType.DMA((n_sems,))]
     scratch += [pltpu.VMEM((4,) + shapes[-1], jnp.float32), pltpu.SemaphoreType.DMA((3,)),
                 pltpu.SemaphoreType.DMA((4,))]
+    y_quarter = width >> 3
+    scratch += [pltpu.VMEM((4, 4, rows, y_quarter), jnp.float32),
+                pltpu.SemaphoreType.DMA((3 * n_chunks,)), pltpu.SemaphoreType.DMA((4 * n_chunks,))]
     vmem = pl.BlockSpec(memory_space=pltpu.VMEM)
     out = pl.pallas_call(
         functools.partial(fused_kernel, depth_scale, n_rounds, lane_rounds, n_chunks),

time: 72.3 us -> 61.5 us (0.85)
  Pallas kernels: 66.7 us -> 55.5 us
    pallas_call x1, Pallas kernels: 66.7 us -> 55.5 us  [render_composite(): pl.pallas_call(functools.partial(fused_kernel, depth_scale, n_rounds, lan...]
where the time goes in v9:
time: 61.5 us; the launch traced here: 60.7 us
  Pallas kernels  55.5 us (90%)
  local copies, waits for them, and re-layouts  4.47 us (7%)
  other arithmetic  0.69 us (1%)
    pallas_call x1, Pallas kernels, render_composite(): pl.pallas_call(functools.partial(fused_kernel, depth_scale, n_rounds, lan...  55.5 us
    unnamed x5, local copies, waits for them, and re-layouts  3.81 us

profile of v9, /device:TPU:8, one launch (start us, length us, event | category | flops | bytes accessed | tf_op | source)
XLA Modules:
  0.0 60.7 jit_solution(12077987985885202162)
XLA Ops:
  0.0 0.7 %broadcast_in_dim.4 = bf16[1,256]{1,0:T(2,128)(2,1)S(1)} reshape(bf16[256]{0:T(256)(128)(2,1)} %param.7) | data formatting | bytes 1024 | tf_op jit(solution)/shard_map/broadcast_in_dim | solution.py:459
  0.7 0.7 %fusion.3.table_ref = f32[8,256]{1,0:T(8,128)S(1)} fusion(bf16[1,256]{1,0:T(2,128)(2,1)S(1)} %broadcast_in_dim.4, bf16[3,256]{1,0:T(4,128)(2,1)} %param.6), kind=kLoop, calls=%fused_computation.4 | loop fusion | flops 14336 | bytes 10240 | tf_op jit(solution)/shard_map/concatenate | solution.py:460
  1.3 0.0 copy-start
  1.4 1.6 %copy-done = f32[2,128,2048]{2,1,0:T(8,128)S(1)} copy-done((f32[2,128,2048]{2,1,0:T(8,128)S(1)}, f32[2,128,2048]{2,1,0:T(8,128)}, u32[]{:S(2)}) %copy-start) | copy-done | bytes 2097176
  2.9 0.0 copy-start.1
  2.9 1.6 %copy-done.1 = s32[2,128,2048]{2,1,0:T(8,128)S(1)} copy-done((s32[2,128,2048]{2,1,0:T(8,128)S(1)}, s32[2,128,2048]{2,1,0:T(8,128)}, u32[]{:S(2)}) %copy-start.1) | copy-done | bytes 2097176
  4.5 55.5 %shard_map.46 = f32[4,32,128]{2,1,0:T(8,128)S(1)} custom-call(f32[8,256]{1,0:T(8,128)S(1)} %fusion.3.table_ref, f32[2,128,2048]{2,1,0:T(8,128)S(1)} %copy-done, s32[2,128,2048]{2,1,0:T(8,128)S(1)} %copy-done.1), custom_call_target="tpu_custom_call" | custom-call | tf_op jit(solution)/shard_map/pallas_call | solution.py:443
  60.0 0.6 %copy.6 = f32[4,128,32]{1,2,0:T(8,128)} copy(f32[4,128,32]{1,2,0:T(8,128)S(1)} %bitcast.1) | data formatting | bytes 131072
Async XLA Ops:
  1.3 1.6 %copy-start = (f32[2,128,2048]{2,1,0:T(8,128)S(1)}, f32[2,128,2048]{2,1,0:T(8,128)}, u32[]{:S(2)}) copy-start(f32[2,128,2048]{2,1,0:T(8,128)} %d_ref.1) | copy-start | bytes 6291460
  2.9 1.6 %copy-start.1 = (s32[2,128,2048]{2,1,0:T(8,128)S(1)}, s32[2,128,2048]{2,1,0:T(8,128)}, u32[]{:S(2)}) copy-start(s32[2,128,2048]{2,1,0:T(8,128)} %b_ref.1) | copy-start | bytes 6291460

commit v10 on v9

--- a/solution.py
+++ b/solution.py
@@ -146,8 +146,9 @@
     lax.fori_loop(0, half // 8, body, 0)
 
 
-def fused_kernel(depth_scale, n_rounds, lane_rounds, n_chunks, table_ref, d_ref, b_ref, out_ref,
-                 img_ref, stash_ref, xp_ref, xn_ref, htop_ref, hbot_ref, halo_send, halo_recv, *scratch):
+def fused_kernel(depth_scale, n_rounds, lane_rounds, n_chunks, colors_ref, ext_ref, d_hbm, b_hbm,
+                 out_ref, d_ref, b_ref, load_sems, img_ref, stash_ref, xp_ref, xn_ref, htop_ref, hbot_ref,
+                 halo_send, halo_recv, *scratch):
     recv = scratch[:n_rounds]
     acc = scratch[n_rounds:2 * n_rounds - 1]
     flip_ref = scratch[2 * n_rounds - 1]
@@ -172,6 +173,17 @@
     extra_nb = jnp.where(odd, has_next, has_prev)
     extra_id = jnp.where(odd, me + 1, me - 1)
 
+    loads = []
+    for c in range(n_chunks):
+        row_sl = pl.ds(c * row_block, row_block)
+        pair = (pltpu.make_async_copy(d_hbm.at[:, row_sl, :], d_ref.at[:, row_sl, :],
+                                      load_sems.at[2 * c]),
+                pltpu.make_async_copy(b_hbm.at[:, row_sl, :], b_ref.at[:, row_sl, :],
+                                      load_sems.at[2 * c + 1]))
+        for copy in pair:
+            copy.start()
+        loads.append(pair)
+
     barrier = pltpu.get_barrier_semaphore()
     for r in range(n_rounds):
         pl.semaphore_signal(barrier, inc=1, device_id=(partners[r], tile), device_id_type=mesh_id)
@@ -211,25 +223,27 @@
             recv_sem=halo_recv.at[idx], device_id=dev, device_id_type=mesh_id))
 
     edge_copies = [
-        halo(has_bot, has_top, d_ref.at[:, pl.ds(rows - 8, 8), :], htop_ref, 0, (me, tile + 1)),
-        halo(has_top, has_bot, d_ref.at[:, pl.ds(0, 8), :], hbot_ref, 1, (me, tile - 1)),
+        halo(has_bot, has_top, d_hbm.at[:, pl.ds(rows - 8, 8), :], htop_ref, 0, (me, tile + 1)),
+        halo(has_top, has_bot, d_hbm.at[:, pl.ds(0, 8), :], hbot_ref, 1, (me, tile - 1)),
     ]
     plane_copies = []
     for c in range(n_chunks):
         row_sl = pl.ds(c * row_block, row_block)
         plane_copies.append((
-            halo(has_next, has_prev, d_ref.at[1, row_sl, :], xp_ref.at[row_sl, :], 2 + 2 * c,
+            halo(has_next, has_prev, d_hbm.at[1, row_sl, :], xp_ref.at[row_sl, :], 2 + 2 * c,
                  (me + 1, tile)),
-            halo(has_prev, has_next, d_ref.at[0, row_sl, :], xn_ref.at[row_sl, :], 3 + 2 * c,
+            halo(has_prev, has_next, d_hbm.at[0, row_sl, :], xn_ref.at[row_sl, :], 3 + 2 * c,
                  (me - 1, tile)),
         ))
     all_halos = edge_copies + [h for pair in plane_copies for h in pair]
     for send_if, _, copy in all_halos:
         pl.when(send_if)(copy.start)
 
+    lookup = jnp.concatenate([colors_ref[...].astype(jnp.float32),
+                              ext_ref[...].astype(jnp.float32)], 0)
     tables = [
-        (jnp.broadcast_to(table_ref[ch:ch + 1, 0:LANES], (8, LANES)),
-         jnp.broadcast_to(table_ref[ch:ch + 1, LANES:2 * LANES], (8, LANES)))
+        (jnp.broadcast_to(lookup[ch:ch + 1, 0:LANES], (8, LANES)),
+         jnp.broadcast_to(lookup[ch:ch + 1, LANES:2 * LANES], (8, LANES)))
         for ch in range(4)
     ]
     look = make_look(tables)
@@ -317,6 +331,11 @@
             start_lane(r + 1, c)
 
     for c in range(n_chunks):
+        loads[c][1].wait()
+        if c == 0:
+            loads[0][0].wait()
+        if c + 1 < n_chunks:
+            loads[c + 1][0].wait()
         lookup_rows(depth_scale, look, b_ref, stash_ref, img_ref, c * row_block, row_block)
         waits = list(plane_copies[c])
         if c == 0:
@@ -409,7 +428,7 @@
         src = dst
 
 
-def render_composite(density, bins, table, depth_scale, n_rounds):
+def render_composite(density, bins, colors, extinction, depth_scale, n_rounds):
     planes, rows, width = density.shape
     lane_rounds = 0
     while (width >> (lane_rounds + 1)) >= LANES and lane_rounds < n_rounds:
@@ -420,6 +439,9 @@
         half = width >> (r + 1)
         shapes.append((4, rows, half) if r < lane_rounds else (4, half, rows))
     scratch = [
+        pltpu.VMEM((planes, rows, width), jnp.float32),
+        pltpu.VMEM((planes, rows, width), jnp.int32),
+        pltpu.SemaphoreType.DMA((2 * n_chunks,)),
         pltpu.VMEM((4, rows, width), jnp.float32),
         pltpu.VMEM((6, rows, width), jnp.float32),
         pltpu.VMEM((rows, width), jnp.float32),
@@ -443,12 +465,12 @@
     out = pl.pallas_call(
         functools.partial(fused_kernel, depth_scale, n_rounds, lane_rounds, n_chunks),
         out_shape=jax.ShapeDtypeStruct(shapes[-1], jnp.float32),
-        in_specs=[vmem] * 3,
+        in_specs=[vmem, vmem, pl.BlockSpec(memory_space=pl.ANY), pl.BlockSpec(memory_space=pl.ANY)],
         out_specs=vmem,
         scratch_shapes=scratch,
         compiler_params=pltpu.CompilerParams(
-            collective_id=0, has_side_effects=True, vmem_limit_bytes=48 * 1024 * 1024),
-    )(table, density, bins)
+            collective_id=0, has_side_effects=True, vmem_limit_bytes=63 * 1024 * 1024),
+    )(colors, extinction, density, bins)
     return jnp.transpose(out, (0, 2, 1))
 
 
@@ -456,9 +478,8 @@
     depth_cells = density.shape[0]
     slab_count = lax.axis_size("depth")
     depth_scale = 0.6 / (depth_cells * slab_count)
-    lookup = jnp.concatenate([colors, extinction[None, :]], 0).astype(jnp.float32)
-    table = jnp.concatenate([lookup, jnp.zeros((4, lookup.shape[1]), jnp.float32)], 0)
-    return render_composite(density, bins, table, depth_scale, slab_count.bit_length() - 1)
+    return render_composite(density, bins, colors, extinction.reshape(1, -1), depth_scale,
+                            slab_count.bit_length() - 1)
 
 
 def solution(mesh):

time: 61.5 us -> 60.8 us (0.989)
  local copies, waits for them, and re-layouts: 4.47 us -> 2.69 us
  Pallas kernels: 55.5 us -> 57.2 us
  other arithmetic: 0.69 us -> 0 us
    unnamed x5 -> x1, local copies, waits for them, and re-layouts: 3.81 us -> 1.47 us
    pallas_call x1, Pallas kernels: 55.5 us -> 57.2 us  [render_composite(): pl.pallas_call(functools.partial(fused_kernel, depth_scale, n_rounds, lan...]
    reshape x0 -> x1, local copies, waits for them, and re-layouts: none -> 1.22 us  [per_device(): extinction.reshape(1, -1)]
    concatenate x1 -> x0, other arithmetic: 0.69 us -> none  [per_device(): jnp.concatenate([lookup, jnp.zeros((4, lookup.shape[1]), jnp.float32)], 0)]
    broadcast_in_dim x1 -> x0, local copies, waits for them, and re-layouts: 0.66 us -> none  [per_device(): extinction[None, :]]
where the time goes in v10:
time: 60.8 us; the launch traced here: 59.9 us
  Pallas kernels  57.2 us (94%)
  local copies, waits for them, and re-layouts  2.69 us (4%)
    pallas_call x1, Pallas kernels, render_composite(): pl.pallas_call(functools.partial(fused_kernel, depth_scale, n_rounds, lan...  57.2 us
    unnamed x1, local copies, waits for them, and re-layouts  1.47 us
    reshape x1, local copies, waits for them, and re-layouts, per_device(): extinction.reshape(1, -1)  1.22 us

profile of v10, /device:TPU:8, one launch (start us, length us, event | category | flops | bytes accessed | tf_op | source)
XLA Modules:
  0.0 59.9 jit_solution(16829128539935052229)
XLA Ops:
  0.0 1.2 %reshape.3.ext_ref = bf16[1,256]{1,0:T(2,128)(2,1)} reshape(bf16[256]{0:T(256)(128)(2,1)} %param.7) | data formatting | bytes 1024 | tf_op jit(solution)/shard_map/reshape | solution.py:481
  1.2 57.2 %shard_map.46 = f32[4,32,128]{2,1,0:T(8,128)} custom-call(bf16[3,256]{1,0:T(4,128)(2,1)} %colors_ref.1, bf16[1,256]{1,0:T(2,128)(2,1)} %reshape.3.ext_ref, f32[2,128,2048]{2,1,0:T(8,128)} %d_hbm.1, s32[2,128,2048]{2,1,0:T(8,128)} %b_hbm.1), custom_call_target="tpu_custom_call" | custom-call | tf_op jit(solution)/shard_map/pallas_call | solution.py:465
  58.4 1.5 %copy.6 = f32[4,128,32]{1,2,0:T(8,128)} copy(f32[4,128,32]{1,2,0:T(8,128)} %bitcast.1) | data formatting | bytes 131072
